TPU v7x, 32 devices: a whole 2x2x4 slice. The times are simulated.
32 devices in a mesh: side: 2 (over y), gx: 4 (over x, core), gy: 4 (over z).
Axes of the slice: x: 2, y: 2, z: 4, core: 2. Of those that a mesh axis runs over, the one named last changes fastest.
Arguments:
- populations: float32 [2, 19, 4, 128, 512], P('side', None, None, 'gx', 'gy'), may hold values from 0.01 to 0.84, as said below
- solid_mask: int32 [2, 4, 128, 512], P('side', None, 'gx', 'gy'), may hold values 0 or 1
- water_sheet: float32 [32, 128, 512], P(None, 'gx', ('side', 'gy')), may hold values from 2 to 12
- current: float32 [128, 512], P('gx', ('side', 'gy')), may hold values from 0.5 to 3
Outputs:
- populations_out: float32 [2, 19, 4, 128, 512], P('side', None, None, 'gx', 'gy')
- sheet_out: float32 [32, 128, 512], P(None, 'gx', ('side', 'gy'))
Inputs may be any that keep to these rules, and one draw needn't show every extreme that they name: `populations`: every population is positive.
All inputs are finite; a program needn't handle non-finite values. No bound on the sum of `solid_mask` on one device may be relied on, other than what follows from the above.
Results may differ from a plain program's by a relative error of at most 0.0003.
Values sent between devices are 32-bit elements; how exact they have to be, the bound alone decides.
No kernel may reach another device: no remote copies, remote signals or barrier semaphores. Data moves between devices by JAX's collectives and lax.ppermute only.
A program may use at most 64 MiB of HBM per device.

v0:
```python
import functools

import jax
import jax.numpy as jnp
from jax import lax
from jax.experimental import pallas as pl
from jax.experimental.pallas import tpu as pltpu
from jax.sharding import PartitionSpec as P

STEPS = 8
SUBSTEPS = 2
HALO = 2 * STEPS
TILE = 8
LANES = 128

velocity_table = (
    (0, 0, 0),
    (1, 0, 0),
    (-1, 0, 0),
    (0, 1, 0),
    (0, -1, 0),
    (0, 0, 1),
    (0, 0, -1),
    (1, 1, 0),
    (-1, -1, 0),
    (1, -1, 0),
    (-1, 1, 0),
    (1, 0, 1),
    (-1, 0, -1),
    (1, 0, -1),
    (-1, 0, 1),
    (0, 1, 1),
    (0, -1, -1),
    (0, 1, -1),
    (0, -1, 1),
)
DIRS = len(velocity_table)
wall_potential = 0.4
uptake_rate = 0.02
drag_rate = 0.03
base_diffusion = 0.05
slope_diffusion = 0.015
ROOT2 = 2.0**0.5

VMEM = pl.BlockSpec(memory_space=pltpu.VMEM)


def uptake(density_row):
    activity = density_row / (1.0 + density_row)
    return 0.043 + activity * (17.18 + activity * (-39.85 + 36.0 * activity))


def spin(tile, shift):
    shift = shift % LANES
    return tile if shift == 0 else pltpu.roll(tile, shift, 1)


def lane_index():
    return lax.broadcasted_iota(jnp.int32, (TILE, LANES), 1)


def run_steps(fields, density_ref, psi_ref, pore_ref, flux_ref, layers, window_rows):
    def step_body(step, carry):
        here = lax.rem(step, 2)
        there = 1 - here
        first = 2 * step

        def potentials(tile, inner):
            row = first + TILE * tile
            rows = pl.ds(row, TILE)
            for z in range(layers):
                parts = [fields[here, i, z, rows, :] for i in range(DIRS)]
                while len(parts) > 1:
                    parts = [a + b for a, b in zip(parts[::2], parts[1::2])] + (
                        [parts[-1]] if len(parts) % 2 else []
                    )
                rho = parts[0]
                density_ref[z, rows, :] = rho
                psi_ref[z, rows, :] = jnp.where(
                    pore_ref[z, rows, :] > 0.5, 1.0 - jnp.exp(-rho), wall_potential
                )
            return inner

        lax.fori_loop(0, (window_rows - 2 * first + TILE - 1) // TILE, potentials, 0)

        def collide(tile, inner):
            row = first + 1 + TILE * tile
            rows = pl.ds(row, TILE)
            up = pl.ds(row + 1, TILE)
            down = pl.ds(row - 1, TILE)
            centre = [psi_ref[z, rows, :] for z in range(layers)]
            plus = [psi_ref[z, up, :] for z in range(layers)]
            minus = [psi_ref[z, down, :] for z in range(layers)]
            slope = [a - b for a, b in zip(plus, minus)]
            pair = [a + b for a, b in zip(plus, minus)]

            def across(values, z, sign):
                above = values[z + 1] if z + 1 < layers else None
                below = values[z - 1] if z > 0 else None
                if above is None and below is None:
                    return jnp.zeros((TILE, LANES), jnp.float32)
                if above is None:
                    return below if sign > 0 else -below
                if below is None:
                    return above
                return above + below if sign > 0 else above - below

            for z in range(layers):
                pull_x = (
                    (slope[z] + slope[z])
                    + across(slope, z, 1)
                    + (spin(slope[z], 1) + spin(slope[z], -1))
                )
                lift = across(centre, z, -1)
                pull_z = (lift + lift) + across(pair, z, -1) + (spin(lift, 1) + spin(lift, -1))
                shell = (centre[z] + centre[z]) + pair[z] + across(centre, z, 1)
                pull_y = spin(shell, -1) - spin(shell, 1)

                rho = density_ref[z, rows, :]
                is_pore = pore_ref[z, rows, :] > 0.5
                f = [fields[here, i, z, rows, :] for i in range(DIRS)]
                total = [None] + [f[i] + f[i + 1] for i in range(1, DIRS, 2)]
                delta = [None] + [f[i] - f[i + 1] for i in range(1, DIRS, 2)]
                moment = []
                for component in range(3):
                    terms = []
                    for k in range(1, 10):
                        factor = velocity_table[2 * k - 1][component]
                        if factor:
                            terms.append((factor, delta[k]))
                    value = terms[0][1]
                    for factor, term in terms[1:]:
                        value = value + term if factor > 0 else value - term
                    moment.append(value)
                pulled = centre[z] * (1.0 / 15.0)
                scale = jnp.where(is_pore, (3.0 / ROOT2) / rho, 0.0)
                u = [
                    (moment[c] + pulled * pull) * scale
                    for c, pull in enumerate((pull_x, pull_y, pull_z))
                ]
                base = 1.0 - (u[0] * u[0] + u[1] * u[1] + u[2] * u[2]) * (1.0 / 3.0)
                a_diag = jnp.where(is_pore, rho * (1.25 / 36.0), 0.0)
                a_axis = a_diag + a_diag
                o_diag = a_diag * ROOT2
                o_axis = a_axis * ROOT2
                keep_even = jnp.where(is_pore, -0.125, 0.5)
                keep_odd = jnp.where(is_pore, -0.125, -0.5)
                fields[there, 0, z, rows, :] = f[0] * (keep_even + keep_even) + base * (
                    a_diag * 12.0
                )
                for k in range(1, 10):
                    i = 2 * k - 1
                    e = velocity_table[i]
                    along = None
                    for component in range(3):
                        if e[component] == 0:
                            continue
                        if along is None:
                            along = u[component]
                        elif e[component] > 0:
                            along = along + u[component]
                        else:
                            along = along - u[component]
                    axis = k <= 3
                    even = total[k] * keep_even + (along * along + base) * (
                        a_axis if axis else a_diag
                    )
                    odd = delta[k] * keep_odd + along * (o_axis if axis else o_diag)
                    for j, sign, post in ((i, 1, even + odd), (i + 1, -1, even - odd)):
                        other = i + 1 if j == i else i
                        shift_x, shift_y, shift_z = (sign * v for v in e)
                        if z + shift_z < 0:
                            inflow = flux_ref[rows, :] * (1.0 / 3.0 if axis else 1.0 / 6.0)
                            fields[there, other, z, rows, :] = post - inflow
                        elif z + shift_z >= layers:
                            fields[there, other, z, rows, :] = post
                        else:
                            fields[there, j, z + shift_z, pl.ds(row + shift_x, TILE), :] = spin(
                                post, shift_y
                            )
            return inner

        lax.fori_loop(0, (window_rows - 2 - 2 * first + TILE - 1) // TILE, collide, 0)
        return carry

    lax.fori_loop(0, STEPS, step_body, 0)


def set_flux(fields, water_of, flux_ref, window_rows):
    def flux_rows(tile, carry):
        rows = pl.ds(TILE * tile, TILE)
        rho = fields[0, 0, 0, rows, :]
        for i in range(1, DIRS):
            rho = rho + fields[0, i, 0, rows, :]
        flux_ref[rows, :] = uptake_rate * (uptake(rho) - flux_ref[rows, :])
        return carry

    lax.fori_loop(0, window_rows // TILE, flux_rows, 0)


def middle_kernel(f_ref, mask_ref, water_ref, low_ref, high_ref, clow_ref, chigh_ref, out_ref,
                  fields, density_ref, psi_ref, pore_ref, flux_ref):
    layers, height = f_ref.shape[1], f_ref.shape[2]
    centre = slice(HALO, HALO + height)
    after = slice(HALO + height, 2 * HALO + height)

    def load(i, carry):
        for z in range(layers):
            fields[0, i, z, :HALO, :] = low_ref[i, z]
            fields[0, i, z, centre, :] = f_ref[i, z]
            fields[0, i, z, after, :] = high_ref[i, z]
        return carry

    lax.fori_loop(0, DIRS, load, 0)
    for z in range(layers):
        pore_ref[z, :HALO, :] = low_ref[DIRS, z]
        pore_ref[z, centre, :] = mask_ref[z].astype(jnp.float32)
        pore_ref[z, after, :] = high_ref[DIRS, z]
    flux_ref[:HALO, :] = clow_ref[DIRS + 1]
    flux_ref[centre, :] = water_ref[0]
    flux_ref[after, :] = chigh_ref[DIRS + 1]
    window_rows = height + 2 * HALO
    set_flux(fields, None, flux_ref, window_rows)
    run_steps(fields, density_ref, psi_ref, pore_ref, flux_ref, layers, window_rows)

    def save(i, carry):
        for z in range(layers):
            out_ref[i, z] = fields[STEPS % 2, i, z, centre, :]
        return carry

    lax.fori_loop(0, DIRS, save, 0)


def edge_kernel(f_ref, mask_ref, water_ref, low_ref, high_ref, left_ref, right_ref, clow_ref,
                chigh_ref, middle_ref, out_ref, fields, density_ref, psi_ref, pore_ref, flux_ref):
    layers, height = f_ref.shape[1], f_ref.shape[2]
    lane = lane_index()
    two = 2 * HALO
    low_tiles = HALO // TILE
    mid_tiles = height // TILE
    half_tiles = mid_tiles // 2
    half_lanes = LANES // 2
    right_at, left_at = two, LANES - 3 * HALO

    def join(own, left, right):
        outer = jnp.where(lane < two, spin(own, two), spin(own, -two))
        halo = jnp.where(lane < half_lanes, right, left)
        return jnp.where((lane < two) | (lane >= LANES - two), outer, halo)

    def own_tile(i, z, tile, kind):
        if tile < low_tiles:
            return low_ref[i, z, TILE * tile : TILE * (tile + 1), :]
        if tile < low_tiles + mid_tiles:
            t = tile - low_tiles
            if kind == "mask":
                return mask_ref[z, TILE * t : TILE * (t + 1), :].astype(jnp.float32)
            return f_ref[i, z, TILE * t : TILE * (t + 1), :]
        t = tile - low_tiles - mid_tiles
        return high_ref[i, z, TILE * t : TILE * (t + 1), :]

    def halo_tiles(i, z, tile):
        if low_tiles <= tile < low_tiles + mid_tiles:
            t = tile - low_tiles
            at = half_lanes * (t // half_tiles) + HALO * z
            rows = slice(TILE * (t % half_tiles), TILE * (t % half_tiles) + TILE)
            return (
                spin(left_ref[i, rows, :], left_at - at),
                spin(right_ref[i, rows, :], right_at - at),
            )
        ref = clow_ref if tile < low_tiles else chigh_ref
        t = tile if tile < low_tiles else tile - low_tiles - mid_tiles
        both = ref[i, TILE * t : TILE * (t + 1), :]
        return spin(both, left_at - HALO * z), spin(both, right_at - half_lanes - HALO * z)

    tiles = 2 * low_tiles + mid_tiles

    def load(i, carry):
        for z in range(layers):
            for tile in range(tiles):
                rows = slice(TILE * tile, TILE * (tile + 1))
                fields[0, i, z, rows, :] = join(own_tile(i, z, tile, "f"), *halo_tiles(i, z, tile))
        return carry

    lax.fori_loop(0, DIRS, load, 0)
    for z in range(layers):
        for tile in range(tiles):
            rows = slice(TILE * tile, TILE * (tile + 1))
            pore_ref[z, rows, :] = join(
                own_tile(DIRS, z, tile, "mask"), *halo_tiles(DIRS, z, tile)
            )
    for tile in range(tiles):
        rows = slice(TILE * tile, TILE * (tile + 1))
        if tile < low_tiles:
            own, extra = (clow_ref[DIRS + 1 + k, rows, :] for k in range(2))
        elif tile < low_tiles + mid_tiles:
            t = tile - low_tiles
            own, extra = (water_ref[k, TILE * t : TILE * (t + 1), :] for k in range(2))
        else:
            t = tile - low_tiles - mid_tiles
            own, extra = (chigh_ref[DIRS + 1 + k, TILE * t : TILE * (t + 1), :] for k in range(2))
        flux_ref[rows, :] = join(own, spin(extra, -two), spin(extra, two))
    window_rows = height + 2 * HALO
    set_flux(fields, None, flux_ref, window_rows)
    run_steps(fields, density_ref, psi_ref, pore_ref, flux_ref, layers, window_rows)

    def save(i, carry):
        for z in range(layers):
            for t in range(mid_tiles):
                rows = slice(TILE * t, TILE * (t + 1))
                edge = fields[STEPS % 2, i, z, HALO + TILE * t : HALO + TILE * (t + 1), :]
                edge = jnp.where(lane < half_lanes, spin(edge, two), spin(edge, -two))
                inside = (lane >= HALO) & (lane < LANES - HALO)
                out_ref[i, z, rows, :] = jnp.where(inside, middle_ref[i, z, rows, :], edge)
        return carry

    lax.fori_loop(0, DIRS, save, 0)


def window_scratch(layers, rows):
    padded = rows + TILE
    return [
        pltpu.VMEM((2, DIRS, layers, padded, LANES), jnp.float32),
        pltpu.VMEM((layers, padded, LANES), jnp.float32),
        pltpu.VMEM((layers, padded, LANES), jnp.float32),
        pltpu.VMEM((layers, padded, LANES), jnp.float32),
        pltpu.VMEM((padded, LANES), jnp.float32),
    ]


def strip_kernel(f_ref, mask_ref, left_ref, right_ref):
    layers, height = f_ref.shape[1], f_ref.shape[2]
    lane = lane_index()
    half_rows = height // 2
    half_lanes = LANES // 2

    def pack(i, read):
        for t in range(half_rows // TILE):
            rows = slice(TILE * t, TILE * (t + 1))
            first = last = None
            for h in range(2):
                for z in range(layers):
                    tile = read(z, slice(half_rows * h + TILE * t, half_rows * h + TILE * (t + 1)))
                    at = half_lanes * h + HALO * z
                    one = spin(tile, at)
                    two = spin(tile, at + HALO)
                    mine = lane >= at
                    first = one if first is None else jnp.where(mine, one, first)
                    last = two if last is None else jnp.where(mine, two, last)
            left_ref[i, rows, :] = first
            right_ref[i, rows, :] = last

    def each(i, carry):
        pack(i, lambda z, rows: f_ref[i, z, rows, :])
        return carry

    lax.fori_loop(0, DIRS, each, 0)
    pack(DIRS, lambda z, rows: mask_ref[z, rows, :].astype(jnp.float32))


def corner_kernel(left_ref, right_ref, water_ref, up_ref, down_ref):
    half_lanes = LANES // 2
    lane = lane_index()
    tiles = left_ref.shape[1] // TILE

    def each(i, carry):
        for t in range(tiles):
            rows = slice(TILE * t, TILE * (t + 1))
            left, right = left_ref[i, rows, :], right_ref[i, rows, :]
            up_ref[i, rows, :] = jnp.where(lane < half_lanes, spin(left, half_lanes), right)
            down_ref[i, rows, :] = jnp.where(lane < half_lanes, left, spin(right, half_lanes))
        return carry

    lax.fori_loop(0, DIRS + 1, each, 0)
    height = water_ref.shape[1]
    for k in range(2):
        up_ref[DIRS + 1 + k] = water_ref[k, height - HALO :, :]
        down_ref[DIRS + 1 + k] = water_ref[k, :HALO, :]


def whole_call(kernel, outs, scratch, flops, bytes_accessed):
    return pl.pallas_call(
        kernel,
        out_shape=outs,
        in_specs=None,
        out_specs=jax.tree.map(lambda _: VMEM, outs),
        scratch_shapes=scratch,
        cost_estimate=pl.CostEstimate(
            flops=flops, bytes_accessed=bytes_accessed, transcendentals=0
        ),
    )


def sheet_substep(water, current_rows, inflow_anode, inflow_cathode):
    diffusivity = base_diffusion + slope_diffusion * water
    face_z = (
        -0.5 * (diffusivity[1:] + diffusivity[:-1]) * (water[1:] - water[:-1])
        + drag_rate * current_rows[None] * water[:-1]
    )
    change = jnp.concatenate([inflow_anode[None], face_z]) - jnp.concatenate(
        [face_z, -inflow_cathode[None]]
    )
    return water + change


def ring(axis, shift):
    count = lax.axis_size(axis)
    return [(i, (i + shift) % count) for i in range(count)]


def on_device(populations, solid_mask, water_sheet, current):
    lattice = populations[0]
    solids = solid_mask[0]
    layers, height, width = lattice.shape[1:]
    groups = lax.axis_size(("side", "gy"))
    gy_count = lax.axis_size("gy")
    sub = width // groups
    f32 = jnp.float32
    mask_values = solids.astype(f32)[None]

    def rows_of(cut):
        return jnp.concatenate([lattice[:, :, cut], mask_values[:, :, cut]])

    low = lax.ppermute(rows_of(slice(height - HALO, height)), "gx", ring("gx", 1))
    high = lax.ppermute(rows_of(slice(0, HALO)), "gx", ring("gx", -1))

    strip = jax.ShapeDtypeStruct((DIRS + 1, height // 2, LANES), f32)
    send_left, send_right = pl.pallas_call(
        strip_kernel, out_shape=(strip, strip),
        in_specs=[VMEM, VMEM], out_specs=(VMEM, VMEM),
    )(lattice, solids)
    left = lax.ppermute(send_right, "gy", ring("gy", 1))
    right = lax.ppermute(send_left, "gy", ring("gy", -1))

    surface = jnp.sum(lattice[:, 0], axis=0)
    ends = jnp.stack([water_sheet[0], water_sheet[-1]])
    own = ends.reshape(2, height, gy_count, sub).transpose(0, 2, 1, 3)
    me = lax.axis_index(("side", "gy"))
    extra = jnp.where(me < groups // 2, jnp.roll(own, -1, axis=1), jnp.roll(own, 1, axis=1))
    to_sheet = surface.reshape(height, groups, sub).transpose(1, 0, 2)
    payload = jnp.stack(
        [own.reshape(groups, height, sub), extra.reshape(groups, height, sub), to_sheet], axis=1
    ).reshape(groups, 3 * height * sub // LANES, LANES)
    got = lax.all_to_all(payload, ("side", "gy"), split_axis=0, concat_axis=0, tiled=True)
    got = got.reshape(groups, 3, height, sub)
    water_here = got[:, :2].transpose(1, 2, 0, 3).reshape(2, height, width)
    halves = got[:, 2].reshape(2, gy_count, height, sub).transpose(0, 2, 1, 3)
    halves = halves.reshape(2, height, gy_count * sub)
    inflow_anode = uptake_rate * (uptake(halves[0]) - water_sheet[0])
    inflow_cathode = uptake_rate * (uptake(halves[1]) - water_sheet[-1])
    water = water_sheet
    for repeat in range(SUBSTEPS):
        water = sheet_substep(water, current, inflow_anode, inflow_cathode)

    corner = jax.ShapeDtypeStruct((DIRS + 3, HALO, LANES), f32)
    send_up, send_down = pl.pallas_call(
        corner_kernel, out_shape=(corner, corner),
        in_specs=[VMEM] * 3, out_specs=(VMEM, VMEM),
    )(left, right, water_here)
    corner_low = lax.ppermute(send_up, "gx", ring("gx", 1))
    corner_high = lax.ppermute(send_down, "gx", ring("gx", -1))

    window = height + 2 * HALO
    result = jax.ShapeDtypeStruct(lattice.shape, f32)
    cost = pl.CostEstimate(flops=200 * 8 * 4 * 52 * 128, bytes_accessed=8 << 20, transcendentals=0)
    middle = pl.pallas_call(
        middle_kernel, out_shape=result, in_specs=[VMEM] * 7, out_specs=VMEM,
        scratch_shapes=window_scratch(layers, window), cost_estimate=cost,
    )(lattice, solids, water_here, low, high, corner_low, corner_high)
    out = pl.pallas_call(
        edge_kernel, out_shape=result, in_specs=[VMEM] * 10, out_specs=VMEM,
        scratch_shapes=window_scratch(layers, window), cost_estimate=cost,
    )(lattice, solids, water_here, low, high, left, right, corner_low, corner_high, middle)
    return (out[None], water)


def solution(mesh):
    in_specs = (
        P("side", None, None, "gx", "gy"),
        P("side", None, "gx", "gy"),
        P(None, "gx", ("side", "gy")),
        P("gx", ("side", "gy")),
    )
    out_specs = (P("side", None, None, "gx", "gy"), P(None, "gx", ("side", "gy")))
    return jax.shard_map(
        on_device, mesh=mesh, in_specs=in_specs, out_specs=out_specs, check_vma=False
    )
```

profile of v0, /device:TPU:1, one launch (start us, length us, event | category | flops | bytes accessed | tf_op | source)
XLA Modules:
  0.0 109.0 jit_solution(1759012599070231535)
XLA Ops:
  0.6 0.7 fusion.12
  1.5 1.1 %slice_reduce_fusion = f32[32,128]{1,0:T(8,128)S(1)} fusion(f32[19,4,32,128]{3,2,1,0:T(8,128)} %bitcast.23), kind=kLoop, calls=%fused_computation.21 | loop fusion | flops 73728 | bytes 327680 | tf_op jit(solution)/shard_map/reduce_sum | solution.py:434
  2.8 0.2 copy.34
  2.9 0.8 reshape.122
  3.7 6.4 %all-to-all-start = ((f32[8,12,128]{2,1,0:T(8,128)}), f32[8,12,128]{2,1,0:T(8,128)S(1)}, u32[]{:S(2)}, u32[]{:S(2)}) async-start(f32[8,12,128]{2,1,0:T(8,128)} %reshape.122), calls=%async_computation | async-start | bytes 131072 | tf_op jit(solution)/shard_map/all_to_all | solution.py:443
  10.1 0.2 fusion.11
  10.3 0.7 copy-done.4
  10.9 0.9 pad_maximum_fusion.4
  11.8 2.1 %collective-permute-start = (f32[20,4,16,128]{3,2,1,0:T(8,128)}, f32[20,4,16,128]{3,2,1,0:T(8,128)S(1)}, u32[]{:S(2)}, u32[]{:S(2)}) collective-permute-start(f32[20,4,16,128]{3,2,1,0:T(8,128)} %pad_maximum_fusion.4), channel_id=1, source_target_pairs={{0,4},{4,8},{8,12},{12,0},{1,5},{5,9},{9,13},{13,1},{2,6},{6,10},{... | collective-permute-start | bytes 1966088 | tf_op jit(solution)/shard_map/ppermute | solution.py:423
  13.9 0.9 pad_maximum_fusion.5
  14.8 4.0 %shard_map.59 = (f32[20,16,128]{2,1,0:T(8,128)}, f32[20,16,128]{2,1,0:T(8,128)}) custom-call(f32[19,4,32,128]{3,2,1,0:T(8,128)} %bitcast.24, s32[4,32,128]{2,1,0:T(8,128)} %bitcast.29), custom_call_target="tpu_custom_call" | custom-call | tf_op jit(solution)/shard_map/pallas_call | solution.py:427
  18.8 1.7 %collective-permute-start.2 = (f32[20,16,128]{2,1,0:T(8,128)}, f32[20,16,128]{2,1,0:T(8,128)S(1)}, u32[]{:S(2)}, u32[]{:S(2)}) collective-permute-start(f32[20,16,128]{2,1,0:T(8,128)} %get-tuple-element.6), channel_id=1, source_target_pairs={{0,1},{1,2},{2,3},{3,0},{4,5},{5,6},{6,7},{7,4},{8,9},{9,10},{10,1... | collective-permute-start | bytes 491528 | tf_op jit(solution)/shard_map/ppermute | solution.py:431
  20.5 1.8 %collective-permute-start.3 = (f32[20,16,128]{2,1,0:T(8,128)}, f32[20,16,128]{2,1,0:T(8,128)S(1)}, u32[]{:S(2)}, u32[]{:S(2)}) collective-permute-start(f32[20,16,128]{2,1,0:T(8,128)} %get-tuple-element.7), channel_id=1, source_target_pairs={{0,3},{1,0},{2,1},{3,2},{4,7},{5,4},{6,5},{7,6},{8,11},{9,8},{10,9... | collective-permute-start | bytes 491528 | tf_op jit(solution)/shard_map/ppermute | solution.py:432
  22.4 0.1 fusion.9
  22.6 0.2 reshape.123
  22.8 0.1 copy.35
  22.9 0.7 copy.38.water_ref
  23.9 0.2 multiply_add_fusion
  24.0 0.1 fusion.5
  24.1 2.3 %collective-permute-done.2.left_ref = f32[20,16,128]{2,1,0:T(8,128)S(1)} collective-permute-done((f32[20,16,128]{2,1,0:T(8,128)}, f32[20,16,128]{2,1,0:T(8,128)S(1)}, u32[]{:S(2)}, u32[]{:S(2)}) %collective-permute-start.2) | collective-permute-done | bytes 163872 | tf_op jit(solution)/shard_map/ppermute | solution.py:431
  26.5 3.5 %collective-permute-done.3.right_ref = f32[20,16,128]{2,1,0:T(8,128)S(1)} collective-permute-done((f32[20,16,128]{2,1,0:T(8,128)}, f32[20,16,128]{2,1,0:T(8,128)S(1)}, u32[]{:S(2)}, u32[]{:S(2)}) %collective-permute-start.3) | collective-permute-done | bytes 163872 | tf_op jit(solution)/shard_map/ppermute | solution.py:432
  30.0 0.7 copy-done.8
  30.7 3.2 %shard_map.60 = (f32[22,16,128]{2,1,0:T(8,128)}, f32[22,16,128]{2,1,0:T(8,128)}) custom-call(f32[20,16,128]{2,1,0:T(8,128)} %copy-done.7, f32[20,16,128]{2,1,0:T(8,128)} %copy-done.8, f32[2,32,128]{2,1,0:T(8,128)} %copy.38.water_ref), custom_call_target="tpu_custom_call" | custom-call | tf_op jit(solution)/shard_map/pallas_call | solution.py:455
  33.8 1.0 collective-permute-start.4
  34.8 0.9 fusion.3
  35.7 2.0 %collective-permute-done.4.clow_ref = f32[22,16,128]{2,1,0:T(8,128)S(1)} collective-permute-done((f32[22,16,128]{2,1,0:T(8,128)}, f32[22,16,128]{2,1,0:T(8,128)S(1)}, u32[]{:S(2)}, u32[]{:S(2)}) %collective-permute-start.4) | collective-permute-done | bytes 180256 | tf_op jit(solution)/shard_map/ppermute | solution.py:459
  37.7 3.3 %collective-permute-done.5.chigh_ref = f32[22,16,128]{2,1,0:T(8,128)S(1)} collective-permute-done((f32[22,16,128]{2,1,0:T(8,128)}, f32[22,16,128]{2,1,0:T(8,128)S(1)}, u32[]{:S(2)}, u32[]{:S(2)}) %collective-permute-start.5) | collective-permute-done | bytes 180256 | tf_op jit(solution)/shard_map/ppermute | solution.py:460
  41.1 0.7 copy-done.6
  41.7 0.2 copy-done.2
  42.0 0.8 copy-done.3
  42.8 30.0 %shard_map.61.middle_ref = f32[19,4,32,128]{3,2,1,0:T(8,128)} custom-call(f32[19,4,32,128]{3,2,1,0:T(8,128)} %bitcast.25, s32[4,32,128]{2,1,0:T(8,128)} %bitcast.30, f32[2,32,128]{2,1,0:T(8,128)} %copy.38.water_ref, f32[20,4,16,128]{3,2,1,0:T(8,128)} %copy-done.2, f32[20,4,16,128]{3,2,1,0:T(8,128)} %copy-done.3, f32[22,16,128]{2,1,0:T(8,128)} %copy-done.5, ...), custom_call_target="tpu_custom_call" | custom-call | flops 42598400 | bytes 8388608 | tf_op jit(solution)/shard_map/pallas_call | solution.py:465
  72.8 36.2 %shard_map.62 = f32[19,4,32,128]{3,2,1,0:T(8,128)} custom-call(f32[19,4,32,128]{3,2,1,0:T(8,128)} %bitcast.26, s32[4,32,128]{2,1,0:T(8,128)} %bitcast.31, f32[2,32,128]{2,1,0:T(8,128)} %copy.38.water_ref, f32[20,4,16,128]{3,2,1,0:T(8,128)} %copy-done.2, f32[20,4,16,128]{3,2,1,0:T(8,128)} %copy-done.3, f32[20,16,128]{2,1,0:T(8,128)} %copy-done.7, ...), custom_call_target="tpu_custom_call" | custom-call | flops 42598400 | bytes 8388608 | tf_op jit(solution)/shard_map/pallas_call | solution.py:469
  (38 shorter events, 0.7 us)
Async XLA Ops:
  1.5 8.6 %copy-start = (f32[1,19,4,32,128]{4,3,2,1,0:T(8,128)S(1)}, f32[1,19,4,32,128]{4,3,2,1,0:T(8,128)}, u32[]{:S(2)}) copy-start(f32[1,19,4,32,128]{4,3,2,1,0:T(8,128)} %param.4) | copy-start | bytes 3735556
  3.7 18.8 %all-to-all-start = ((f32[8,12,128]{2,1,0:T(8,128)}), f32[8,12,128]{2,1,0:T(8,128)S(1)}, u32[]{:S(2)}, u32[]{:S(2)}) async-start(f32[8,12,128]{2,1,0:T(8,128)} %reshape.122), calls=%async_computation | async-start | bytes 131072 | tf_op jit(solution)/shard_map/all_to_all | solution.py:443
  10.1 0.8 copy-start.4
  11.8 29.2 %collective-permute-start = (f32[20,4,16,128]{3,2,1,0:T(8,128)}, f32[20,4,16,128]{3,2,1,0:T(8,128)S(1)}, u32[]{:S(2)}, u32[]{:S(2)}) collective-permute-start(f32[20,4,16,128]{3,2,1,0:T(8,128)} %pad_maximum_fusion.4), channel_id=1, source_target_pairs={{0,4},{4,8},{8,12},{12,0},{1,5},{5,9},{9,13},{13,1},{2,6},{6,10},{... | collective-permute-start | bytes 1966088 | tf_op jit(solution)/shard_map/ppermute | solution.py:423
  13.9 8.4 %copy-start.1 = (f32[32,32,64]{2,1,0:T(8,128)S(1)}, f32[32,32,64]{2,1,0:T(8,128)}, u32[]{:S(2)}) copy-start(f32[32,32,64]{2,1,0:T(8,128)} %param.6) | copy-start | bytes 786436
  14.8 7.6 %copy-start.9 = (f32[32,64]{1,0:T(8,128)S(1)}, f32[32,64]{1,0:T(8,128)}, u32[]{:S(2)}) copy-start(f32[32,64]{1,0:T(8,128)} %param.7) | copy-start | bytes 24580
  14.8 26.3 %collective-permute-start.1 = (f32[20,4,16,128]{3,2,1,0:T(8,128)}, f32[20,4,16,128]{3,2,1,0:T(8,128)S(1)}, u32[]{:S(2)}, u32[]{:S(2)}) collective-permute-start(f32[20,4,16,128]{3,2,1,0:T(8,128)} %pad_maximum_fusion.5), channel_id=1, source_target_pairs={{0,12},{4,0},{8,4},{12,8},{1,13},{5,1},{9,5},{13,9},{2,14},{6,2},{... | collective-permute-start | bytes 1966088 | tf_op jit(solution)/shard_map/ppermute | solution.py:424
  18.8 7.7 %collective-permute-start.2 = (f32[20,16,128]{2,1,0:T(8,128)}, f32[20,16,128]{2,1,0:T(8,128)S(1)}, u32[]{:S(2)}, u32[]{:S(2)}) collective-permute-start(f32[20,16,128]{2,1,0:T(8,128)} %get-tuple-element.6), channel_id=1, source_target_pairs={{0,1},{1,2},{2,3},{3,0},{4,5},{5,6},{6,7},{7,4},{8,9},{9,10},{10,1... | collective-permute-start | bytes 491528 | tf_op jit(solution)/shard_map/ppermute | solution.py:431
  20.5 9.5 %collective-permute-start.3 = (f32[20,16,128]{2,1,0:T(8,128)}, f32[20,16,128]{2,1,0:T(8,128)S(1)}, u32[]{:S(2)}, u32[]{:S(2)}) collective-permute-start(f32[20,16,128]{2,1,0:T(8,128)} %get-tuple-element.7), channel_id=1, source_target_pairs={{0,3},{1,0},{2,1},{3,2},{4,7},{5,4},{6,5},{7,6},{8,11},{9,8},{10,9... | collective-permute-start | bytes 491528 | tf_op jit(solution)/shard_map/ppermute | solution.py:432
  26.5 3.5 %copy-start.7 = (f32[20,16,128]{2,1,0:T(8,128)}, f32[20,16,128]{2,1,0:T(8,128)S(1)}, u32[]{:S(2)}) copy-start(f32[20,16,128]{2,1,0:T(8,128)S(1)} %collective-permute-done.2.left_ref) | copy-start | bytes 491524
  30.0 0.7 copy-start.8
  33.8 3.9 %collective-permute-start.4 = (f32[22,16,128]{2,1,0:T(8,128)}, f32[22,16,128]{2,1,0:T(8,128)S(1)}, u32[]{:S(2)}, u32[]{:S(2)}) collective-permute-start(f32[22,16,128]{2,1,0:T(8,128)} %get-tuple-element.8), channel_id=1, source_target_pairs={{0,4},{4,8},{8,12},{12,0},{1,5},{5,9},{9,13},{13,1},{2,6},{6,10},{... | collective-permute-start | bytes 540680 | tf_op jit(solution)/shard_map/ppermute | solution.py:459
  34.8 6.2 %collective-permute-start.5 = (f32[22,16,128]{2,1,0:T(8,128)}, f32[22,16,128]{2,1,0:T(8,128)S(1)}, u32[]{:S(2)}, u32[]{:S(2)}) collective-permute-start(f32[22,16,128]{2,1,0:T(8,128)} %get-tuple-element.9), channel_id=1, source_target_pairs={{0,12},{4,0},{8,4},{12,8},{1,13},{5,1},{9,5},{13,9},{2,14},{6,2},{... | collective-permute-start | bytes 540680 | tf_op jit(solution)/shard_map/ppermute | solution.py:460
  37.7 3.3 %copy-start.5 = (f32[22,16,128]{2,1,0:T(8,128)}, f32[22,16,128]{2,1,0:T(8,128)S(1)}, u32[]{:S(2)}) copy-start(f32[22,16,128]{2,1,0:T(8,128)S(1)} %collective-permute-done.4.clow_ref) | copy-start | bytes 540676
  41.0 0.7 copy-start.6
  41.1 0.9 copy-start.2
  42.0 0.8 copy-start.3
where the time goes:
time: 109 us
  Pallas kernels  73.4 us (67%)
  starting transfers between devices  12.9 us (12%)
  waiting for transfers between devices  11.2 us (10%)
  local copies, waits for them, and re-layouts  6.34 us (6%)
  other arithmetic  4.34 us (4%)
    pallas_call x1, Pallas kernels, on_device(): pl.pallas_call(edge_kernel, out_shape=result, in_specs=[VMEM] * 10, out_s...  36.2 us
    pallas_call x1, Pallas kernels, on_device(): pl.pallas_call(middle_kernel, out_shape=result, in_specs=[VMEM] * 7, out_...  30 us
    all_to_all x1, starting transfers between devices, on_device(): lax.all_to_all(payload, ('side', 'gy'), split_axis=0, concat_axis=0, tile...  6.37 us
    pallas_call x1, Pallas kernels, on_device(): pl.pallas_call(strip_kernel, out_shape=(strip, strip), in_specs=[VMEM, VM...  3.97 us
    ppermute x1, waiting for transfers between devices, on_device(): right = lax.ppermute(send_left, 'gy', ring('gy', -1))  3.52 us
    ppermute x1, waiting for transfers between devices, on_device(): corner_high = lax.ppermute(send_down, 'gx', ring('gx', -1))  3.33 us
    pallas_call x1, Pallas kernels, on_device(): pl.pallas_call(corner_kernel, out_shape=(corner, corner), in_specs=[VMEM]...  3.17 us
    unnamed x20, local copies, waits for them, and re-layouts  3.06 us
  transfers between devices with their start and end apart: 7, of which 4 were waited for; matrix products, arithmetic and copies ran while one was open for 4% of the time, Pallas kernels for 7%

commit v1 on v0

v1 whole, which is shorter than its diff:
```python
import functools

import jax
import jax.numpy as jnp
from jax import lax
from jax.experimental import pallas as pl
from jax.experimental.pallas import tpu as pltpu
from jax.sharding import PartitionSpec as P

STEPS = 8
SUBSTEPS = 2
HALO = 2 * STEPS
TILE = 8
LANES = 128

velocity_table = (
    (0, 0, 0),
    (1, 0, 0),
    (-1, 0, 0),
    (0, 1, 0),
    (0, -1, 0),
    (0, 0, 1),
    (0, 0, -1),
    (1, 1, 0),
    (-1, -1, 0),
    (1, -1, 0),
    (-1, 1, 0),
    (1, 0, 1),
    (-1, 0, -1),
    (1, 0, -1),
    (-1, 0, 1),
    (0, 1, 1),
    (0, -1, -1),
    (0, 1, -1),
    (0, -1, 1),
)
DIRS = len(velocity_table)
wall_potential = 0.4
uptake_rate = 0.02
drag_rate = 0.03
base_diffusion = 0.05
slope_diffusion = 0.015
ROOT2 = 2.0**0.5

VMEM = pl.BlockSpec(memory_space=pltpu.VMEM)


def uptake(density_row):
    activity = density_row / (1.0 + density_row)
    return 0.043 + activity * (17.18 + activity * (-39.85 + 36.0 * activity))


def spin(tile, shift):
    shift = shift % LANES
    return tile if shift == 0 else pltpu.roll(tile, shift, 1)


def lane_index():
    return lax.broadcasted_iota(jnp.int32, (TILE, LANES), 1)


def set_pairs(values, row, z, even_ref, odd_ref, rest_ref, density_ref, psi_ref, pore):
    rows = pl.ds(row, TILE)
    if rest_ref is not None:
        rest_ref[z, rows, :] = values[0]
    rho = values[0]
    partial = []
    for k in range(9):
        one, two = values[2 * k + 1], values[2 * k + 2]
        both = one + two
        even_ref[k, z, rows, :] = both
        odd_ref[k, z, rows, :] = one - two
        partial.append(both)
    while len(partial) > 1:
        partial = [a + b for a, b in zip(partial[::2], partial[1::2])] + (
            [partial[-1]] if len(partial) % 2 else []
        )
    rho = rho + partial[0]
    density_ref[z, rows, :] = rho
    psi_ref[z, rows, :] = jnp.where(pore > 0.5, 1.0 - jnp.exp(-rho), wall_potential)
    return rho


def run_steps(refs, layers, window_rows):
    (posts, sets, pull_ref, pore_ref, flux_ref) = refs
    spare = window_rows + 2 * TILE

    def across(values, z, sign):
        above = values[z + 1] if z + 1 < layers else None
        below = values[z - 1] if z > 0 else None
        if above is None and below is None:
            return jnp.zeros((TILE, LANES), jnp.float32)
        if above is None:
            return below if sign > 0 else -below
        if below is None:
            return above
        return above + below if sign > 0 else above - below

    def gather(row, target):
        even_ref, odd_ref, density_ref, psi_ref = target
        rows = pl.ds(row, TILE)
        for z in range(layers):
            values = []
            for i in range(DIRS):
                _, shift_y, shift_z = velocity_table[i]
                reflected = z - shift_z < 0 or z - shift_z >= layers
                values.append(spin(posts[i, z, rows, :], 0 if reflected else shift_y))
            set_pairs(values, row, z, even_ref, odd_ref, None, density_ref, psi_ref, pore_ref[z, rows, :])

    def pull(row, source):
        psi_ref = source[3]
        rows = pl.ds(row, TILE)
        centre = [psi_ref[z, rows, :] for z in range(layers)]
        plus = [psi_ref[z, pl.ds(row + 1, TILE), :] for z in range(layers)]
        minus = [psi_ref[z, pl.ds(row - 1, TILE), :] for z in range(layers)]
        slope = [a - b for a, b in zip(plus, minus)]
        pair = [a + b for a, b in zip(plus, minus)]
        for z in range(layers):
            lift = across(centre, z, -1)
            shell = (centre[z] + centre[z]) + pair[z] + across(centre, z, 1)
            pull_ref[0, z, rows, :] = (
                (slope[z] + slope[z]) + across(slope, z, 1) + (spin(slope[z], 1) + spin(slope[z], -1))
            )
            pull_ref[1, z, rows, :] = spin(shell, -1) - spin(shell, 1)
            pull_ref[2, z, rows, :] = (
                (lift + lift) + across(pair, z, -1) + (spin(lift, 1) + spin(lift, -1))
            )

    def collide(row, source):
        even_ref, odd_ref, density_ref, psi_ref = source
        rows = pl.ds(row, TILE)
        for z in range(layers):
            rho = density_ref[z, rows, :]
            is_pore = pore_ref[z, rows, :] > 0.5
            delta = [None] + [odd_ref[k, z, rows, :] for k in range(9)]
            pulled = psi_ref[z, rows, :] * (1.0 / 15.0)
            scale = jnp.where(is_pore, (3.0 / ROOT2) / rho, 0.0)
            u = []
            for component in range(3):
                value = None
                for k in range(1, 10):
                    factor = velocity_table[2 * k - 1][component]
                    if factor:
                        if value is None:
                            value = delta[k]
                        else:
                            value = value + delta[k] if factor > 0 else value - delta[k]
                u.append((value + pulled * pull_ref[component, z, rows, :]) * scale)
            base = 1.0 - (u[0] * u[0] + u[1] * u[1] + u[2] * u[2]) * (1.0 / 3.0)
            a_diag = jnp.where(is_pore, rho * (1.25 / 36.0), 0.0)
            a_axis = a_diag + a_diag
            o_diag = a_diag * ROOT2
            o_axis = a_axis * ROOT2
            keep_even = jnp.where(is_pore, -0.125, 0.5)
            keep_odd = jnp.where(is_pore, -0.125, -0.5)
            posts[0, z, rows, :] = posts[0, z, rows, :] * (keep_even + keep_even) + base * (a_diag * 12.0)
            for k in range(1, 10):
                i = 2 * k - 1
                e = velocity_table[i]
                along = None
                for component in range(3):
                    if e[component] == 0:
                        continue
                    if along is None:
                        along = u[component]
                    elif e[component] > 0:
                        along = along + u[component]
                    else:
                        along = along - u[component]
                axis = k <= 3
                even = even_ref[k - 1, z, rows, :] * keep_even + (along * along + base) * (
                    a_axis if axis else a_diag
                )
                odd = delta[k] * keep_odd + along * (o_axis if axis else o_diag)
                for j, sign, post in ((i, 1, even + odd), (i + 1, -1, even - odd)):
                    other = i + 1 if j == i else i
                    shift_x, shift_y, shift_z = (sign * v for v in e)
                    if z + shift_z < 0:
                        inflow = flux_ref[rows, :] * (1.0 / 3.0 if axis else 1.0 / 6.0)
                        posts[other, z, rows, :] = post - inflow
                    elif z + shift_z >= layers:
                        posts[other, z, rows, :] = post
                    else:
                        posts[j, z + shift_z, pl.ds(row + shift_x, TILE), :] = post

    def tiles_of(step):
        return (window_rows - 2 - 4 * step + TILE - 1) // TILE

    def two_steps(pair, carry):
        for half in range(2):
            step = 2 * pair + half
            first = 2 * step + 1
            here, there = sets[half], sets[1 - half]
            before = step - 1
            last = jnp.where(step == 0, spare, 2 * before + TILE * (tiles_of(before) - 1))
            gather(last, here)
            pull(first, here)
            pull(first + TILE, here)
            collide(first, here)

            def turn(tile, inner, first=first, here=here, there=there):
                row = first + TILE * tile
                pull(row + TILE, here)
                gather(row - 1 - TILE, there)
                collide(row, here)
                return inner

            lax.fori_loop(1, tiles_of(step), turn, 0)
        return carry

    lax.fori_loop(0, STEPS // 2, two_steps, 0)
    gather(2 * (STEPS - 1) + TILE * (tiles_of(STEPS - 1) - 1), sets[STEPS % 2])


def start_flux(rho, row, flux_ref):
    rows = pl.ds(row, TILE)
    flux_ref[rows, :] = uptake_rate * (uptake(rho) - flux_ref[rows, :])


def begin(read, read_pore, row, layers, refs):
    (posts, sets, pull_ref, pore_ref, flux_ref) = refs
    even_ref, odd_ref, density_ref, psi_ref = sets[0]
    for z in range(layers):
        pore = read_pore(z)
        pore_ref[z, pl.ds(row, TILE), :] = pore
        values = [read(i, z) for i in range(DIRS)]
        rho = set_pairs(values, row, z, even_ref, odd_ref, posts.at[0], density_ref, psi_ref, pore)
        if z == 0:
            start_flux(rho, row, flux_ref)


def finish(write, refs, layers, height):
    (posts, sets, pull_ref, pore_ref, flux_ref) = refs
    even_ref, odd_ref = sets[STEPS % 2][:2]

    def tile_out(t, carry):
        rows = pl.ds(HALO + TILE * t, TILE)
        for z in range(layers):
            write(0, z, t, posts[0, z, rows, :])
            for k in range(9):
                even, odd = even_ref[k, z, rows, :], odd_ref[k, z, rows, :]
                write(2 * k + 1, z, t, (even + odd) * 0.5)
                write(2 * k + 2, z, t, (even - odd) * 0.5)
        return carry

    lax.fori_loop(0, height // TILE, tile_out, 0)


def regroup(scratch):
    posts, e0, o0, d0, p0, e1, o1, d1, p1, pull_ref, pore_ref, flux_ref = scratch
    return posts, ((e0, o0, d0, p0), (e1, o1, d1, p1)), pull_ref, pore_ref, flux_ref


def window_scratch(layers, rows):
    padded = rows + 3 * TILE

    def one(*lead):
        return pltpu.VMEM(lead + (padded, LANES), jnp.float32)

    state = [one(9, layers), one(9, layers), one(layers), one(layers)]
    return [one(DIRS, layers)] + state + state + [one(3, layers), one(layers), one()]


def middle_kernel(f_ref, mask_ref, water_ref, low_ref, high_ref, clow_ref, chigh_ref, out_ref, *scratch):
    refs = regroup(scratch)
    flux_ref = refs[4]
    layers, height = f_ref.shape[1], f_ref.shape[2]
    flux_ref[:HALO, :] = clow_ref[DIRS + 1]
    flux_ref[HALO : HALO + height, :] = water_ref[0]
    flux_ref[HALO + height : 2 * HALO + height, :] = chigh_ref[DIRS + 1]

    def outer(ref, start):
        def tile_in(t, carry):
            rows = pl.ds(pl.multiple_of(TILE * t, TILE), TILE)
            begin(lambda i, z: ref[i, z, rows, :], lambda z: ref[DIRS, z, rows, :], start + TILE * t, layers, refs)
            return carry

        lax.fori_loop(0, HALO // TILE, tile_in, 0)

    outer(low_ref, 0)

    def tile_in(t, carry):
        rows = pl.ds(pl.multiple_of(TILE * t, TILE), TILE)
        begin(lambda i, z: f_ref[i, z, rows, :], lambda z: mask_ref[z, rows, :].astype(jnp.float32),
              HALO + TILE * t, layers, refs)
        return carry

    lax.fori_loop(0, height // TILE, tile_in, 0)
    outer(high_ref, HALO + height)
    run_steps(refs, layers, height + 2 * HALO)

    def write(i, z, t, value):
        out_ref[i, z, pl.ds(pl.multiple_of(TILE * t, TILE), TILE), :] = value

    finish(write, refs, layers, height)


def edge_kernel(f_ref, mask_ref, water_ref, low_ref, high_ref, left_ref, right_ref, clow_ref,
                chigh_ref, middle_ref, out_ref, *scratch):
    refs = regroup(scratch)
    flux_ref = refs[4]
    layers, height = f_ref.shape[1], f_ref.shape[2]
    lane = lane_index()
    move = 3 * HALO
    left_at = 2 * HALO
    low_tiles = HALO // TILE
    mid_tiles = height // TILE
    half_tiles = mid_tiles // 2
    half_lanes = LANES // 2
    at_end = lane >= LANES - 2 * HALO
    at_left = (lane >= left_at) & (lane < left_at + HALO)
    at_right = lane < HALO

    def join(own, left, right):
        return jnp.where(at_end, own, jnp.where(at_right, right, jnp.where(at_left, left, spin(own, move))))

    for tile in range(2 * low_tiles + mid_tiles):
        if low_tiles <= tile < low_tiles + mid_tiles:
            t = tile - low_tiles
            own_rows = slice(TILE * t, TILE * (t + 1))
            rows = slice(TILE * (t % half_tiles), TILE * (t % half_tiles) + TILE)
            first = half_lanes * (t // half_tiles)

            def halo(i, z, rows=rows, first=first):
                at = first + HALO * z
                return spin(left_ref[i, rows, :], left_at - at), spin(right_ref[i, rows, :], -at)

            def read(i, z, own_rows=own_rows, halo=halo):
                return join(f_ref[i, z, own_rows, :], *halo(i, z))

            def read_pore(z, own_rows=own_rows, halo=halo):
                return join(mask_ref[z, own_rows, :].astype(jnp.float32), *halo(DIRS, z))

            own, extra = (water_ref[k, own_rows, :] for k in range(2))
        else:
            t = tile if tile < low_tiles else tile - low_tiles - mid_tiles
            own_ref, corner_ref = (low_ref, clow_ref) if tile < low_tiles else (high_ref, chigh_ref)
            rows = slice(TILE * t, TILE * (t + 1))

            def read(i, z, rows=rows, own_ref=own_ref, corner_ref=corner_ref):
                both = corner_ref[i, rows, :]
                return join(own_ref[i, z, rows, :], spin(both, left_at - HALO * z),
                            spin(both, -half_lanes - HALO * z))

            def read_pore(z, read=read):
                return read(DIRS, z)

            own, extra = (corner_ref[DIRS + 1 + k, rows, :] for k in range(2))
        flux_ref[TILE * tile : TILE * (tile + 1), :] = join(own, spin(extra, move), extra)
        begin(read, read_pore, TILE * tile, layers, refs)
    run_steps(refs, layers, height + 2 * HALO)
    inside = (lane >= HALO) & (lane < LANES - HALO)

    def write(i, z, t, value):
        rows = pl.ds(pl.multiple_of(TILE * t, TILE), TILE)
        edge = jnp.where(lane < half_lanes, spin(value, -move), value)
        out_ref[i, z, rows, :] = jnp.where(inside, middle_ref[i, z, rows, :], edge)

    finish(write, refs, layers, height)


def strip_kernel(f_ref, mask_ref, left_ref, right_ref):
    layers, height = f_ref.shape[1], f_ref.shape[2]
    lane = lane_index()
    half_rows = height // 2
    half_lanes = LANES // 2

    def pack(i, read):
        for t in range(half_rows // TILE):
            rows = slice(TILE * t, TILE * (t + 1))
            first = last = None
            for h in range(2):
                for z in range(layers):
                    tile = read(z, slice(half_rows * h + TILE * t, half_rows * h + TILE * (t + 1)))
                    at = half_lanes * h + HALO * z
                    one = spin(tile, at)
                    two = spin(tile, at + HALO)
                    mine = lane >= at
                    first = one if first is None else jnp.where(mine, one, first)
                    last = two if last is None else jnp.where(mine, two, last)
            left_ref[i, rows, :] = first
            right_ref[i, rows, :] = last

    for i in range(DIRS):
        pack(i, lambda z, rows, i=i: f_ref[i, z, rows, :])
    pack(DIRS, lambda z, rows: mask_ref[z, rows, :].astype(jnp.float32))


def corner_kernel(left_ref, right_ref, water_ref, up_ref, down_ref):
    half_lanes = LANES // 2
    lane = lane_index()
    tiles = left_ref.shape[1] // TILE

    for i in range(DIRS + 1):
        for t in range(tiles):
            rows = slice(TILE * t, TILE * (t + 1))
            left, right = left_ref[i, rows, :], right_ref[i, rows, :]
            up_ref[i, rows, :] = jnp.where(lane < half_lanes, spin(left, half_lanes), right)
            down_ref[i, rows, :] = jnp.where(lane < half_lanes, left, spin(right, half_lanes))
    height = water_ref.shape[1]
    for k in range(2):
        up_ref[DIRS + 1 + k] = water_ref[k, height - HALO :, :]
        down_ref[DIRS + 1 + k] = water_ref[k, :HALO, :]


def sheet_substep(water, current_rows, inflow_anode, inflow_cathode):
    diffusivity = base_diffusion + slope_diffusion * water
    face_z = (
        -0.5 * (diffusivity[1:] + diffusivity[:-1]) * (water[1:] - water[:-1])
        + drag_rate * current_rows[None] * water[:-1]
    )
    change = jnp.concatenate([inflow_anode[None], face_z]) - jnp.concatenate(
        [face_z, -inflow_cathode[None]]
    )
    return water + change


def ring(axis, shift):
    count = lax.axis_size(axis)
    return [(i, (i + shift) % count) for i in range(count)]


def on_device(populations, solid_mask, water_sheet, current):
    lattice = populations[0]
    solids = solid_mask[0]
    layers, height, width = lattice.shape[1:]
    groups = lax.axis_size(("side", "gy"))
    gy_count = lax.axis_size("gy")
    sub = width // groups
    f32 = jnp.float32
    mask_values = solids.astype(f32)[None]

    def rows_of(cut):
        return jnp.concatenate([lattice[:, :, cut], mask_values[:, :, cut]])

    low = lax.ppermute(rows_of(slice(height - HALO, height)), "gx", ring("gx", 1))
    high = lax.ppermute(rows_of(slice(0, HALO)), "gx", ring("gx", -1))

    strip = jax.ShapeDtypeStruct((DIRS + 1, height // 2, LANES), f32)
    send_left, send_right = pl.pallas_call(
        strip_kernel, out_shape=(strip, strip),
        in_specs=[VMEM, VMEM], out_specs=(VMEM, VMEM),
    )(lattice, solids)
    left = lax.ppermute(send_right, "gy", ring("gy", 1))
    right = lax.ppermute(send_left, "gy", ring("gy", -1))

    surface = jnp.sum(lattice[:, 0], axis=0)
    ends = jnp.stack([water_sheet[0], water_sheet[-1]])
    own = ends.reshape(2, height, gy_count, sub).transpose(0, 2, 1, 3)
    me = lax.axis_index(("side", "gy"))
    extra = jnp.where(me < groups // 2, jnp.roll(own, -1, axis=1), jnp.roll(own, 1, axis=1))
    to_sheet = surface.reshape(height, groups, sub).transpose(1, 0, 2)
    payload = jnp.stack(
        [own.reshape(groups, height, sub), extra.reshape(groups, height, sub), to_sheet], axis=1
    ).reshape(groups, 3 * height * sub // LANES, LANES)
    got = lax.all_to_all(payload, ("side", "gy"), split_axis=0, concat_axis=0, tiled=True)
    got = got.reshape(groups, 3, height, sub)
    water_here = got[:, :2].transpose(1, 2, 0, 3).reshape(2, height, width)
    halves = got[:, 2].reshape(2, gy_count, height, sub).transpose(0, 2, 1, 3)
    halves = halves.reshape(2, height, gy_count * sub)
    inflow_anode = uptake_rate * (uptake(halves[0]) - water_sheet[0])
    inflow_cathode = uptake_rate * (uptake(halves[1]) - water_sheet[-1])
    water = water_sheet
    for repeat in range(SUBSTEPS):
        water = sheet_substep(water, current, inflow_anode, inflow_cathode)

    corner = jax.ShapeDtypeStruct((DIRS + 3, HALO, LANES), f32)
    send_up, send_down = pl.pallas_call(
        corner_kernel, out_shape=(corner, corner),
        in_specs=[VMEM] * 3, out_specs=(VMEM, VMEM),
    )(left, right, water_here)
    corner_low = lax.ppermute(send_up, "gx", ring("gx", 1))
    corner_high = lax.ppermute(send_down, "gx", ring("gx", -1))

    window = height + 2 * HALO
    result = jax.ShapeDtypeStruct(lattice.shape, f32)
    cost = pl.CostEstimate(flops=200 * 8 * 4 * 52 * 128, bytes_accessed=8 << 20, transcendentals=0)
    middle = pl.pallas_call(
        middle_kernel, out_shape=result, in_specs=[VMEM] * 7, out_specs=VMEM,
        scratch_shapes=window_scratch(layers, window), cost_estimate=cost,
    )(lattice, solids, water_here, low, high, corner_low, corner_high)
    out = pl.pallas_call(
        edge_kernel, out_shape=result, in_specs=[VMEM] * 10, out_specs=VMEM,
        scratch_shapes=window_scratch(layers, window), cost_estimate=cost,
    )(lattice, solids, water_here, low, high, left, right, corner_low, corner_high, middle)
    return (out[None], water)


def solution(mesh):
    in_specs = (
        P("side", None, None, "gx", "gy"),
        P("side", None, "gx", "gy"),
        P(None, "gx", ("side", "gy")),
        P("gx", ("side", "gy")),
    )
    out_specs = (P("side", None, None, "gx", "gy"), P(None, "gx", ("side", "gy")))
    return jax.shard_map(
        on_device, mesh=mesh, in_specs=in_specs, out_specs=out_specs, check_vma=False
    )
```

time: 109 us -> 74.7 us (0.69)
  Pallas kernels: 73.4 us -> 38.6 us
    pallas_call x1, Pallas kernels: 36.2 us -> 18.2 us  [on_device(): pl.pallas_call(edge_kernel, out_shape=result, in_specs=[VMEM] * 10, out_s...]
    pallas_call x1, Pallas kernels: 30 us -> 15.8 us  [on_device(): pl.pallas_call(middle_kernel, out_shape=result, in_specs=[VMEM] * 7, out_...]
    pallas_call x1, Pallas kernels: 3.97 us -> 2.68 us  [on_device(): pl.pallas_call(strip_kernel, out_shape=(strip, strip), in_specs=[VMEM, VM...]
    pallas_call x1, Pallas kernels: 3.17 us -> 1.89 us  [on_device(): pl.pallas_call(corner_kernel, out_shape=(corner, corner), in_specs=[VMEM]...]
  transfers between devices with their start and end apart: 7 -> 7, of which waited for: 4 -> 4; matrix products, arithmetic and copies ran while one was open for 4% -> 6% of each run, Pallas kernels for 7% -> 6%
where the time goes in v1:
time: 74.7 us; the launch traced here: 74.2 us
  Pallas kernels  38.6 us (52%)
  starting transfers between devices  12.9 us (17%)
  waiting for transfers between devices  11.2 us (15%)
  local copies, waits for them, and re-layouts  6.34 us (8%)
  other arithmetic  4.34 us (6%)
  between operations  0.84 us (1%)
    pallas_call x1, Pallas kernels, on_device(): pl.pallas_call(edge_kernel, out_shape=result, in_specs=[VMEM] * 10, out_s...  18.2 us
    pallas_call x1, Pallas kernels, on_device(): pl.pallas_call(middle_kernel, out_shape=result, in_specs=[VMEM] * 7, out_...  15.8 us
    all_to_all x1, starting transfers between devices, on_device(): lax.all_to_all(payload, ('side', 'gy'), split_axis=0, concat_axis=0, tile...  6.37 us
    ppermute x1, waiting for transfers between devices, on_device(): right = lax.ppermute(send_left, 'gy', ring('gy', -1))  3.52 us
    ppermute x1, waiting for transfers between devices, on_device(): corner_high = lax.ppermute(send_down, 'gx', ring('gx', -1))  3.33 us
    unnamed x20, local copies, waits for them, and re-layouts  3.06 us
    pallas_call x1, Pallas kernels, on_device(): pl.pallas_call(strip_kernel, out_shape=(strip, strip), in_specs=[VMEM, VM...  2.68 us
    ppermute x1, waiting for transfers between devices, on_device(): left = lax.ppermute(send_right, 'gy', ring('gy', 1))  2.35 us
  transfers between devices with their start and end apart: 7, of which 4 were waited for; matrix products, arithmetic and copies ran while one was open for 6% of the time, Pallas kernels for 6%

profile of v1, /device:TPU:1, one launch (start us, length us, event | category | flops | bytes accessed | tf_op | source)
XLA Modules:
  0.0 74.2 jit_solution(14113902132108101781)
XLA Ops:
  0.6 0.7 fusion.12
  1.5 1.1 %slice_reduce_fusion = f32[32,128]{1,0:T(8,128)S(1)} fusion(f32[19,4,32,128]{3,2,1,0:T(8,128)} %bitcast.23), kind=kLoop, calls=%fused_computation.21 | loop fusion | flops 73728 | bytes 327680 | tf_op jit(solution)/shard_map/reduce_sum | solution.py:447
  2.8 0.2 copy.34
  2.9 0.8 %reshape.122 = f32[8,12,128]{2,1,0:T(8,128)} reshape(f32[8,3,32,16]{3,2,1,0:T(8,128)S(1)} %copy.34) | data formatting | bytes 98304 | tf_op jit(solution)/shard_map/reshape | solution.py:455
  3.7 6.4 %all-to-all-start = ((f32[8,12,128]{2,1,0:T(8,128)}), f32[8,12,128]{2,1,0:T(8,128)S(1)}, u32[]{:S(2)}, u32[]{:S(2)}) async-start(f32[8,12,128]{2,1,0:T(8,128)} %reshape.122), calls=%async_computation | async-start | bytes 131072 | tf_op jit(solution)/shard_map/all_to_all | solution.py:456
  10.1 0.2 fusion.11
  10.3 0.7 copy-done.4
  10.9 0.9 %pad_maximum_fusion.4 = f32[20,4,16,128]{3,2,1,0:T(8,128)} fusion(f32[1,4,16,128]{3,2,1,0:T(8,128)S(1)} %get-tuple-element.21, f32[19,4,16,128]{3,2,1,0:T(8,128)S(1)} %get-tuple-element.13), kind=kLoop, calls=%fused_computation.4 | loop fusion | flops 163840 | bytes 1310720 | tf_op jit(solution)/shard_map/concatenate | solution.py:434
  11.8 2.1 %collective-permute-start = (f32[20,4,16,128]{3,2,1,0:T(8,128)}, f32[20,4,16,128]{3,2,1,0:T(8,128)S(1)}, u32[]{:S(2)}, u32[]{:S(2)}) collective-permute-start(f32[20,4,16,128]{3,2,1,0:T(8,128)} %pad_maximum_fusion.4), channel_id=1, source_target_pairs={{0,4},{4,8},{8,12},{12,0},{1,5},{5,9},{9,13},{13,1},{2,6},{6,10},{... | collective-permute-start | bytes 1966088 | tf_op jit(solution)/shard_map/ppermute | solution.py:436
  13.9 0.9 %pad_maximum_fusion.5 = f32[20,4,16,128]{3,2,1,0:T(8,128)} fusion(f32[1,4,16,128]{3,2,1,0:T(8,128)S(1)} %get-tuple-element.20, f32[19,4,16,128]{3,2,1,0:T(8,128)S(1)} %get-tuple-element.12), kind=kLoop, calls=%fused_computation.5 | loop fusion | flops 163840 | bytes 1310720 | tf_op jit(solution)/shard_map/concatenate | solution.py:434
  14.8 2.7 %shard_map.59 = (f32[20,16,128]{2,1,0:T(8,128)}, f32[20,16,128]{2,1,0:T(8,128)}) custom-call(f32[19,4,32,128]{3,2,1,0:T(8,128)} %bitcast.24, s32[4,32,128]{2,1,0:T(8,128)} %bitcast.29), custom_call_target="tpu_custom_call" | custom-call | tf_op jit(solution)/shard_map/pallas_call | solution.py:440
  17.5 1.7 %collective-permute-start.2 = (f32[20,16,128]{2,1,0:T(8,128)}, f32[20,16,128]{2,1,0:T(8,128)S(1)}, u32[]{:S(2)}, u32[]{:S(2)}) collective-permute-start(f32[20,16,128]{2,1,0:T(8,128)} %get-tuple-element.6), channel_id=1, source_target_pairs={{0,1},{1,2},{2,3},{3,0},{4,5},{5,6},{6,7},{7,4},{8,9},{9,10},{10,1... | collective-permute-start | bytes 491528 | tf_op jit(solution)/shard_map/ppermute | solution.py:444
  19.2 1.8 %collective-permute-start.3 = (f32[20,16,128]{2,1,0:T(8,128)}, f32[20,16,128]{2,1,0:T(8,128)S(1)}, u32[]{:S(2)}, u32[]{:S(2)}) collective-permute-start(f32[20,16,128]{2,1,0:T(8,128)} %get-tuple-element.7), channel_id=1, source_target_pairs={{0,3},{1,0},{2,1},{3,2},{4,7},{5,4},{6,5},{7,6},{8,11},{9,8},{10,9... | collective-permute-start | bytes 491528 | tf_op jit(solution)/shard_map/ppermute | solution.py:445
  21.1 0.1 fusion.9
  21.3 0.2 reshape.123
  21.5 0.1 copy.35
  21.6 0.7 copy.38.water_ref
  22.6 0.2 multiply_add_fusion
  22.7 0.1 fusion.5
  22.9 2.3 %collective-permute-done.2.left_ref = f32[20,16,128]{2,1,0:T(8,128)S(1)} collective-permute-done((f32[20,16,128]{2,1,0:T(8,128)}, f32[20,16,128]{2,1,0:T(8,128)S(1)}, u32[]{:S(2)}, u32[]{:S(2)}) %collective-permute-start.2) | collective-permute-done | bytes 163872 | tf_op jit(solution)/shard_map/ppermute | solution.py:444
  25.2 3.5 %collective-permute-done.3.right_ref = f32[20,16,128]{2,1,0:T(8,128)S(1)} collective-permute-done((f32[20,16,128]{2,1,0:T(8,128)}, f32[20,16,128]{2,1,0:T(8,128)S(1)}, u32[]{:S(2)}, u32[]{:S(2)}) %collective-permute-start.3) | collective-permute-done | bytes 163872 | tf_op jit(solution)/shard_map/ppermute | solution.py:445
  28.7 0.7 copy-done.8
  29.4 1.9 %shard_map.60 = (f32[22,16,128]{2,1,0:T(8,128)}, f32[22,16,128]{2,1,0:T(8,128)}) custom-call(f32[20,16,128]{2,1,0:T(8,128)} %copy-done.7, f32[20,16,128]{2,1,0:T(8,128)} %copy-done.8, f32[2,32,128]{2,1,0:T(8,128)} %copy.38.water_ref), custom_call_target="tpu_custom_call" | custom-call | tf_op jit(solution)/shard_map/pallas_call | solution.py:468
  31.3 1.0 %collective-permute-start.4 = (f32[22,16,128]{2,1,0:T(8,128)}, f32[22,16,128]{2,1,0:T(8,128)S(1)}, u32[]{:S(2)}, u32[]{:S(2)}) collective-permute-start(f32[22,16,128]{2,1,0:T(8,128)} %get-tuple-element.8), channel_id=1, source_target_pairs={{0,4},{4,8},{8,12},{12,0},{1,5},{5,9},{9,13},{13,1},{2,6},{6,10},{... | collective-permute-start | bytes 540680 | tf_op jit(solution)/shard_map/ppermute | solution.py:472
  32.3 0.9 %fusion.3 = f32[32,32,64]{2,1,0:T(8,128)} fusion(f32[32,32,64]{2,1,0:T(8,128)S(1)} %get-tuple-element.11, f32[1,32,64]{2,1,0:T(8,128)S(1)} %get-tuple-element.15, f32[1,32,64]{2,1,0:T(8,128)S(1)} %get-tuple-element.14, f32[31,32,64]{2,1,0:T(8,128)S(1)} %fusion.5), kind=kLoop, calls=%fused_computation.9 | loop fusion | flops 262144 | bytes 794624 | tf_op jit(solution)/shard_map/add | solution.py:415
  33.1 2.0 %collective-permute-done.4.clow_ref = f32[22,16,128]{2,1,0:T(8,128)S(1)} collective-permute-done((f32[22,16,128]{2,1,0:T(8,128)}, f32[22,16,128]{2,1,0:T(8,128)S(1)}, u32[]{:S(2)}, u32[]{:S(2)}) %collective-permute-start.4) | collective-permute-done | bytes 180256 | tf_op jit(solution)/shard_map/ppermute | solution.py:472
  35.1 3.3 %collective-permute-done.5.chigh_ref = f32[22,16,128]{2,1,0:T(8,128)S(1)} collective-permute-done((f32[22,16,128]{2,1,0:T(8,128)}, f32[22,16,128]{2,1,0:T(8,128)S(1)}, u32[]{:S(2)}, u32[]{:S(2)}) %collective-permute-start.5) | collective-permute-done | bytes 180256 | tf_op jit(solution)/shard_map/ppermute | solution.py:473
  38.5 0.7 copy-done.6
  39.2 0.2 copy-done.2
  39.4 0.8 %copy-done.3 = f32[20,4,16,128]{3,2,1,0:T(8,128)} copy-done((f32[20,4,16,128]{3,2,1,0:T(8,128)}, f32[20,4,16,128]{3,2,1,0:T(8,128)S(1)}, u32[]{:S(2)}) %copy-start.3) | copy-done | bytes 655384
  40.2 15.8 %shard_map.61.middle_ref = f32[19,4,32,128]{3,2,1,0:T(8,128)} custom-call(f32[19,4,32,128]{3,2,1,0:T(8,128)} %bitcast.25, s32[4,32,128]{2,1,0:T(8,128)} %bitcast.30, f32[2,32,128]{2,1,0:T(8,128)} %copy.38.water_ref, f32[20,4,16,128]{3,2,1,0:T(8,128)} %copy-done.2, f32[20,4,16,128]{3,2,1,0:T(8,128)} %copy-done.3, f32[22,16,128]{2,1,0:T(8,128)} %copy-done.5, ...), custom_call_target="tpu_custom_call" | custom-call | flops 42598400 | bytes 8388608 | tf_op jit(solution)/shard_map/pallas_call | solution.py:478
  56.0 18.2 %shard_map.62 = f32[19,4,32,128]{3,2,1,0:T(8,128)} custom-call(f32[19,4,32,128]{3,2,1,0:T(8,128)} %bitcast.26, s32[4,32,128]{2,1,0:T(8,128)} %bitcast.31, f32[2,32,128]{2,1,0:T(8,128)} %copy.38.water_ref, f32[20,4,16,128]{3,2,1,0:T(8,128)} %copy-done.2, f32[20,4,16,128]{3,2,1,0:T(8,128)} %copy-done.3, f32[20,16,128]{2,1,0:T(8,128)} %copy-done.7, ...), custom_call_target="tpu_custom_call" | custom-call | flops 42598400 | bytes 8388608 | tf_op jit(solution)/shard_map/pallas_call | solution.py:482
  (38 shorter events, 0.7 us)
Async XLA Ops:
  1.5 8.6 %copy-start = (f32[1,19,4,32,128]{4,3,2,1,0:T(8,128)S(1)}, f32[1,19,4,32,128]{4,3,2,1,0:T(8,128)}, u32[]{:S(2)}) copy-start(f32[1,19,4,32,128]{4,3,2,1,0:T(8,128)} %param.4) | copy-start | bytes 3735556
  3.7 17.5 %all-to-all-start = ((f32[8,12,128]{2,1,0:T(8,128)}), f32[8,12,128]{2,1,0:T(8,128)S(1)}, u32[]{:S(2)}, u32[]{:S(2)}) async-start(f32[8,12,128]{2,1,0:T(8,128)} %reshape.122), calls=%async_computation | async-start | bytes 131072 | tf_op jit(solution)/shard_map/all_to_all | solution.py:456
  10.1 0.8 %copy-start.4 = (s32[1,4,32,128]{3,2,1,0:T(8,128)S(1)}, s32[1,4,32,128]{3,2,1,0:T(8,128)}, u32[]{:S(2)}) copy-start(s32[1,4,32,128]{3,2,1,0:T(8,128)} %param.5) | copy-start | bytes 196612
  11.8 26.6 %collective-permute-start = (f32[20,4,16,128]{3,2,1,0:T(8,128)}, f32[20,4,16,128]{3,2,1,0:T(8,128)S(1)}, u32[]{:S(2)}, u32[]{:S(2)}) collective-permute-start(f32[20,4,16,128]{3,2,1,0:T(8,128)} %pad_maximum_fusion.4), channel_id=1, source_target_pairs={{0,4},{4,8},{8,12},{12,0},{1,5},{5,9},{9,13},{13,1},{2,6},{6,10},{... | collective-permute-start | bytes 1966088 | tf_op jit(solution)/shard_map/ppermute | solution.py:436
  13.9 7.1 %copy-start.1 = (f32[32,32,64]{2,1,0:T(8,128)S(1)}, f32[32,32,64]{2,1,0:T(8,128)}, u32[]{:S(2)}) copy-start(f32[32,32,64]{2,1,0:T(8,128)} %param.6) | copy-start | bytes 786436
  14.8 6.3 %copy-start.9 = (f32[32,64]{1,0:T(8,128)S(1)}, f32[32,64]{1,0:T(8,128)}, u32[]{:S(2)}) copy-start(f32[32,64]{1,0:T(8,128)} %param.7) | copy-start | bytes 24580
  14.8 23.7 %collective-permute-start.1 = (f32[20,4,16,128]{3,2,1,0:T(8,128)}, f32[20,4,16,128]{3,2,1,0:T(8,128)S(1)}, u32[]{:S(2)}, u32[]{:S(2)}) collective-permute-start(f32[20,4,16,128]{3,2,1,0:T(8,128)} %pad_maximum_fusion.5), channel_id=1, source_target_pairs={{0,12},{4,0},{8,4},{12,8},{1,13},{5,1},{9,5},{13,9},{2,14},{6,2},{... | collective-permute-start | bytes 1966088 | tf_op jit(solution)/shard_map/ppermute | solution.py:437
  17.5 7.7 %collective-permute-start.2 = (f32[20,16,128]{2,1,0:T(8,128)}, f32[20,16,128]{2,1,0:T(8,128)S(1)}, u32[]{:S(2)}, u32[]{:S(2)}) collective-permute-start(f32[20,16,128]{2,1,0:T(8,128)} %get-tuple-element.6), channel_id=1, source_target_pairs={{0,1},{1,2},{2,3},{3,0},{4,5},{5,6},{6,7},{7,4},{8,9},{9,10},{10,1... | collective-permute-start | bytes 491528 | tf_op jit(solution)/shard_map/ppermute | solution.py:444
  19.2 9.5 %collective-permute-start.3 = (f32[20,16,128]{2,1,0:T(8,128)}, f32[20,16,128]{2,1,0:T(8,128)S(1)}, u32[]{:S(2)}, u32[]{:S(2)}) collective-permute-start(f32[20,16,128]{2,1,0:T(8,128)} %get-tuple-element.7), channel_id=1, source_target_pairs={{0,3},{1,0},{2,1},{3,2},{4,7},{5,4},{6,5},{7,6},{8,11},{9,8},{10,9... | collective-permute-start | bytes 491528 | tf_op jit(solution)/shard_map/ppermute | solution.py:445
  25.2 3.5 %copy-start.7 = (f32[20,16,128]{2,1,0:T(8,128)}, f32[20,16,128]{2,1,0:T(8,128)S(1)}, u32[]{:S(2)}) copy-start(f32[20,16,128]{2,1,0:T(8,128)S(1)} %collective-permute-done.2.left_ref) | copy-start | bytes 491524
  28.7 0.7 copy-start.8
  31.3 3.9 %collective-permute-start.4 = (f32[22,16,128]{2,1,0:T(8,128)}, f32[22,16,128]{2,1,0:T(8,128)S(1)}, u32[]{:S(2)}, u32[]{:S(2)}) collective-permute-start(f32[22,16,128]{2,1,0:T(8,128)} %get-tuple-element.8), channel_id=1, source_target_pairs={{0,4},{4,8},{8,12},{12,0},{1,5},{5,9},{9,13},{13,1},{2,6},{6,10},{... | collective-permute-start | bytes 540680 | tf_op jit(solution)/shard_map/ppermute | solution.py:472
  32.2 6.2 %collective-permute-start.5 = (f32[22,16,128]{2,1,0:T(8,128)}, f32[22,16,128]{2,1,0:T(8,128)S(1)}, u32[]{:S(2)}, u32[]{:S(2)}) collective-permute-start(f32[22,16,128]{2,1,0:T(8,128)} %get-tuple-element.9), channel_id=1, source_target_pairs={{0,12},{4,0},{8,4},{12,8},{1,13},{5,1},{9,5},{13,9},{2,14},{6,2},{... | collective-permute-start | bytes 540680 | tf_op jit(solution)/shard_map/ppermute | solution.py:473
  35.1 3.3 %copy-start.5 = (f32[22,16,128]{2,1,0:T(8,128)}, f32[22,16,128]{2,1,0:T(8,128)S(1)}, u32[]{:S(2)}) copy-start(f32[22,16,128]{2,1,0:T(8,128)S(1)} %collective-permute-done.4.clow_ref) | copy-start | bytes 540676
  38.5 0.7 copy-start.6
  38.5 0.9 %copy-start.2 = (f32[20,4,16,128]{3,2,1,0:T(8,128)}, f32[20,4,16,128]{3,2,1,0:T(8,128)S(1)}, u32[]{:S(2)}) copy-start(f32[20,4,16,128]{3,2,1,0:T(8,128)S(1)} %collective-permute-done.low_ref) | copy-start | bytes 1966084
  39.4 0.8 %copy-start.3 = (f32[20,4,16,128]{3,2,1,0:T(8,128)}, f32[20,4,16,128]{3,2,1,0:T(8,128)S(1)}, u32[]{:S(2)}) copy-start(f32[20,4,16,128]{3,2,1,0:T(8,128)S(1)} %collective-permute-done.1.high_ref) | copy-start | bytes 1966084

commit v2 on v1

v2 whole, which is shorter than its diff:
```python
import jax
import jax.numpy as jnp
from jax import lax
from jax.experimental import pallas as pl
from jax.experimental.pallas import tpu as pltpu
from jax.sharding import PartitionSpec as P


STEPS = 8
SUBSTEPS = 2
HALO = 2 * STEPS
TILE = 8
LANES = 128
WINDOWS = 2

velocity_table = (
    (0, 0, 0),
    (1, 0, 0),
    (-1, 0, 0),
    (0, 1, 0),
    (0, -1, 0),
    (0, 0, 1),
    (0, 0, -1),
    (1, 1, 0),
    (-1, -1, 0),
    (1, -1, 0),
    (-1, 1, 0),
    (1, 0, 1),
    (-1, 0, -1),
    (1, 0, -1),
    (-1, 0, 1),
    (0, 1, 1),
    (0, -1, -1),
    (0, 1, -1),
    (0, -1, 1),
)
DIRS = len(velocity_table)
wall_potential = 0.4
uptake_rate = 0.02
drag_rate = 0.03
base_diffusion = 0.05
slope_diffusion = 0.015
ROOT2 = 2.0**0.5

VMEM = pl.BlockSpec(memory_space=pltpu.VMEM)


def uptake(density_row):
    activity = density_row / (1.0 + density_row)
    return 0.043 + activity * (17.18 + activity * (-39.85 + 36.0 * activity))


def spin(tile, shift):
    shift = shift % LANES
    return tile if shift == 0 else pltpu.roll(tile, shift, 1)


def lane_index():
    return lax.broadcasted_iota(jnp.int32, (TILE, LANES), 1)


def set_pairs(values, row, z, even_ref, odd_ref, rest_ref, density_ref, psi_ref, pore):
    rows = pl.ds(row, TILE)
    if rest_ref is not None:
        rest_ref[z, rows, :] = values[0]
    rho = values[0]
    partial = []
    for k in range(9):
        one, two = values[2 * k + 1], values[2 * k + 2]
        both = one + two
        even_ref[k, z, rows, :] = both
        odd_ref[k, z, rows, :] = one - two
        partial.append(both)
    while len(partial) > 1:
        partial = [a + b for a, b in zip(partial[::2], partial[1::2])] + (
            [partial[-1]] if len(partial) % 2 else []
        )
    rho = rho + partial[0]
    density_ref[z, rows, :] = rho
    psi_ref[z, rows, :] = jnp.where(pore > 0.5, 1.0 - jnp.exp(-rho), wall_potential)
    return rho


def run_steps(refs, layers, window_rows):
    (posts, sets, pull_ref, pore_ref, flux_ref) = refs
    spare = window_rows + 2 * TILE
    planes = [(w * layers, w * layers + z, z) for w in range(WINDOWS) for z in range(layers)]

    def across(values, base, z, sign):
        above = values[base + z + 1] if z + 1 < layers else None
        below = values[base + z - 1] if z > 0 else None
        if above is None and below is None:
            return jnp.zeros((TILE, LANES), jnp.float32)
        if above is None:
            return below if sign > 0 else -below
        if below is None:
            return above
        return above + below if sign > 0 else above - below

    def gather(row, target):
        even_ref, odd_ref, density_ref, psi_ref = target
        rows = pl.ds(row, TILE)
        for base, p, z in planes:
            values = []
            for i in range(DIRS):
                _, shift_y, shift_z = velocity_table[i]
                reflected = z - shift_z < 0 or z - shift_z >= layers
                values.append(spin(posts[i, p, rows, :], 0 if reflected else shift_y))
            set_pairs(values, row, p, even_ref, odd_ref, None, density_ref, psi_ref, pore_ref[p, rows, :])

    def pull(row, source):
        psi_ref = source[3]
        rows = pl.ds(row, TILE)
        centre = [psi_ref[p, rows, :] for _, p, _ in planes]
        plus = [psi_ref[p, pl.ds(row + 1, TILE), :] for _, p, _ in planes]
        minus = [psi_ref[p, pl.ds(row - 1, TILE), :] for _, p, _ in planes]
        slope = [a - b for a, b in zip(plus, minus)]
        pair = [a + b for a, b in zip(plus, minus)]
        for base, p, z in planes:
            lift = across(centre, base, z, -1)
            shell = (centre[p] + centre[p]) + pair[p] + across(centre, base, z, 1)
            pull_ref[0, p, rows, :] = (
                (slope[p] + slope[p]) + across(slope, base, z, 1) + (spin(slope[p], 1) + spin(slope[p], -1))
            )
            pull_ref[1, p, rows, :] = spin(shell, -1) - spin(shell, 1)
            pull_ref[2, p, rows, :] = (
                (lift + lift) + across(pair, base, z, -1) + (spin(lift, 1) + spin(lift, -1))
            )

    def collide(row, source):
        even_ref, odd_ref, density_ref, psi_ref = source
        rows = pl.ds(row, TILE)
        for base, p, z in planes:
            rho = density_ref[p, rows, :]
            is_pore = pore_ref[p, rows, :] > 0.5
            delta = [None] + [odd_ref[k, p, rows, :] for k in range(9)]
            pulled = psi_ref[p, rows, :] * (1.0 / 15.0)
            scale = jnp.where(is_pore, (3.0 / ROOT2) / rho, 0.0)
            u = []
            for component in range(3):
                value = None
                for k in range(1, 10):
                    factor = velocity_table[2 * k - 1][component]
                    if factor:
                        if value is None:
                            value = delta[k]
                        else:
                            value = value + delta[k] if factor > 0 else value - delta[k]
                u.append((value + pulled * pull_ref[component, p, rows, :]) * scale)
            base = 1.0 - (u[0] * u[0] + u[1] * u[1] + u[2] * u[2]) * (1.0 / 3.0)
            a_diag = jnp.where(is_pore, rho * (1.25 / 36.0), 0.0)
            a_axis = a_diag + a_diag
            o_diag = a_diag * ROOT2
            o_axis = a_axis * ROOT2
            keep_even = jnp.where(is_pore, -0.125, 0.5)
            keep_odd = jnp.where(is_pore, -0.125, -0.5)
            posts[0, p, rows, :] = posts[0, p, rows, :] * (keep_even + keep_even) + base * (a_diag * 12.0)
            for k in range(1, 10):
                i = 2 * k - 1
                e = velocity_table[i]
                along = None
                for component in range(3):
                    if e[component] == 0:
                        continue
                    if along is None:
                        along = u[component]
                    elif e[component] > 0:
                        along = along + u[component]
                    else:
                        along = along - u[component]
                axis = k <= 3
                even = even_ref[k - 1, p, rows, :] * keep_even + (along * along + base) * (
                    a_axis if axis else a_diag
                )
                odd = delta[k] * keep_odd + along * (o_axis if axis else o_diag)
                for j, sign, post in ((i, 1, even + odd), (i + 1, -1, even - odd)):
                    other = i + 1 if j == i else i
                    shift_x, _, shift_z = (sign * v for v in e)
                    if z + shift_z < 0:
                        inflow = flux_ref[p // layers, rows, :] * (1.0 / 3.0 if axis else 1.0 / 6.0)
                        posts[other, p, rows, :] = post - inflow
                    elif z + shift_z >= layers:
                        posts[other, p, rows, :] = post
                    else:
                        posts[j, p + shift_z, pl.ds(row + shift_x, TILE), :] = post

    def tiles_of(step):
        return (window_rows - 2 - 4 * step + TILE - 1) // TILE

    def two_steps(pair, carry):
        for half in range(2):
            step = 2 * pair + half
            first = 2 * step + 1
            here, there = sets[half], sets[1 - half]
            before = step - 1
            last = jnp.where(step == 0, spare, 2 * before + TILE * (tiles_of(before) - 1))
            gather(last, here)
            pull(first, here)
            pull(first + TILE, here)
            collide(first, here)

            def turn(tile, inner, first=first, here=here, there=there):
                row = first + TILE * tile
                pull(row + TILE, here)
                gather(row - 1 - TILE, there)
                collide(row, here)
                return inner

            lax.fori_loop(1, tiles_of(step), turn, 0)
        return carry

    lax.fori_loop(0, STEPS // 2, two_steps, 0)
    gather(2 * (STEPS - 1) + TILE * (tiles_of(STEPS - 1) - 1), sets[STEPS % 2])


def begin(read, read_pore, row, window, layers, refs):
    (posts, sets, _, pore_ref, flux_ref) = refs
    even_ref, odd_ref, density_ref, psi_ref = sets[0]
    rows = pl.ds(row, TILE)
    for z in range(layers):
        p = window * layers + z
        pore = read_pore(z)
        pore_ref[p, rows, :] = pore
        values = [read(i, z) for i in range(DIRS)]
        rho = set_pairs(values, row, p, even_ref, odd_ref, posts.at[0], density_ref, psi_ref, pore)
        if z == 0:
            flux_ref[window, rows, :] = uptake_rate * (uptake(rho) - flux_ref[window, rows, :])


def finish(out_ref, refs, layers, height):
    (posts, sets, _, _, _) = refs
    even_ref, odd_ref = sets[STEPS % 2][:2]
    lane = lane_index()
    inside = (lane >= HALO) & (lane < LANES - HALO)
    move = 3 * HALO

    def tile_out(t, carry):
        rows = pl.ds(HALO + TILE * t, TILE)
        to = pl.ds(pl.multiple_of(TILE * t, TILE), TILE)

        def join(read):
            middle, edge = read(0), read(1)
            edge = jnp.where(lane < LANES // 2, spin(edge, -move), edge)
            return jnp.where(inside, middle, edge)

        for z in range(layers):
            out_ref[0, z, to, :] = join(lambda w: posts[0, w * layers + z, rows, :])
            for k in range(9):
                even = join(lambda w: even_ref[k, w * layers + z, rows, :]) * 0.5
                odd = join(lambda w: odd_ref[k, w * layers + z, rows, :]) * 0.5
                out_ref[2 * k + 1, z, to, :] = even + odd
                out_ref[2 * k + 2, z, to, :] = even - odd
        return carry

    lax.fori_loop(0, height // TILE, tile_out, 0)


def window_scratch(layers, rows):
    padded = rows + 3 * TILE
    planes = WINDOWS * layers

    def one(*lead):
        return pltpu.VMEM(lead + (padded, LANES), jnp.float32)

    state = [one(9, planes), one(9, planes), one(planes), one(planes)]
    return [one(DIRS, planes)] + state + state + [one(3, planes), one(planes), one(WINDOWS)]


def lattice_kernel(f_ref, mask_ref, water_ref, low_ref, high_ref, left_ref, right_ref, clow_ref,
                   chigh_ref, out_ref, *scratch):
    posts, e0, o0, d0, p0, e1, o1, d1, p1, pull_ref, pore_ref, flux_ref = scratch
    refs = posts, ((e0, o0, d0, p0), (e1, o1, d1, p1)), pull_ref, pore_ref, flux_ref
    layers, height = f_ref.shape[1], f_ref.shape[2]
    lane = lane_index()
    move = 3 * HALO
    left_at = 2 * HALO
    low_tiles = HALO // TILE
    mid_tiles = height // TILE
    half_tiles = mid_tiles // 2
    half_lanes = LANES // 2
    at_end = lane >= LANES - 2 * HALO
    at_left = (lane >= left_at) & (lane < left_at + HALO)
    at_right = lane < HALO

    def join(own, left, right):
        return jnp.where(at_end, own, jnp.where(at_right, right, jnp.where(at_left, left, spin(own, move))))

    for tile in range(2 * low_tiles + mid_tiles):
        if low_tiles <= tile < low_tiles + mid_tiles:
            t = tile - low_tiles
            own_rows = slice(TILE * t, TILE * (t + 1))
            rows = slice(TILE * (t % half_tiles), TILE * (t % half_tiles) + TILE)
            first = half_lanes * (t // half_tiles)

            def own_of(i, z, own_rows=own_rows):
                return f_ref[i, z, own_rows, :] if i < DIRS else mask_ref[z, own_rows, :].astype(jnp.float32)

            def halo(i, z, rows=rows, first=first):
                at = first + HALO * z
                return spin(left_ref[i, rows, :], left_at - at), spin(right_ref[i, rows, :], -at)

            own, extra = (water_ref[k, own_rows, :] for k in range(2))
        else:
            t = tile if tile < low_tiles else tile - low_tiles - mid_tiles
            own_ref, corner_ref = (low_ref, clow_ref) if tile < low_tiles else (high_ref, chigh_ref)
            rows = slice(TILE * t, TILE * (t + 1))

            def own_of(i, z, rows=rows, own_ref=own_ref):
                return own_ref[i, z, rows, :]

            def halo(i, z, rows=rows, corner_ref=corner_ref):
                both = corner_ref[i, rows, :]
                return spin(both, left_at - HALO * z), spin(both, -half_lanes - HALO * z)

            own, extra = (corner_ref[DIRS + 1 + k, rows, :] for k in range(2))

        def edge_of(i, z, own_of=own_of, halo=halo):
            return join(own_of(i, z), *halo(i, z))

        flux_ref[0, TILE * tile : TILE * (tile + 1), :] = own
        flux_ref[1, TILE * tile : TILE * (tile + 1), :] = join(own, spin(extra, move), extra)
        begin(own_of, lambda z, f=own_of: f(DIRS, z), TILE * tile, 0, layers, refs)
        begin(edge_of, lambda z, f=edge_of: f(DIRS, z), TILE * tile, 1, layers, refs)
    run_steps(refs, layers, height + 2 * HALO)
    finish(out_ref, refs, layers, height)


def strip_kernel(me_ref, f_ref, mask_ref, ends_ref, left_ref, right_ref, payload_ref):
    layers, height = f_ref.shape[1], f_ref.shape[2]
    lane = lane_index()
    half_rows = height // 2
    half_lanes = LANES // 2

    def pack(i, read):
        for t in range(half_rows // TILE):
            rows = slice(TILE * t, TILE * (t + 1))
            first = last = None
            for h in range(2):
                for z in range(layers):
                    tile = read(z, slice(half_rows * h + TILE * t, half_rows * h + TILE * (t + 1)))
                    at = half_lanes * h + HALO * z
                    one = spin(tile, at)
                    two = spin(tile, at + HALO)
                    mine = lane >= at
                    first = one if first is None else jnp.where(mine, one, first)
                    last = two if last is None else jnp.where(mine, two, last)
            left_ref[i, rows, :] = first
            right_ref[i, rows, :] = last

    for i in range(DIRS):
        pack(i, lambda z, rows, i=i: f_ref[i, z, rows, :])
    pack(DIRS, lambda z, rows: mask_ref[z, rows, :].astype(jnp.float32))

    groups = payload_ref.shape[0]
    peers = groups // 2
    sub = LANES // groups
    tiles = height // TILE
    early = me_ref[0] < peers
    surface = []
    for t in range(tiles):
        rho = f_ref[0, 0, TILE * t : TILE * (t + 1), :]
        for i in range(1, DIRS):
            rho = rho + f_ref[i, 0, TILE * t : TILE * (t + 1), :]
        surface.append(rho)
    for which in range(2):
        ends = [ends_ref[which, TILE * t : TILE * (t + 1), :] for t in range(tiles)]
        for g in range(peers):
            e = which * peers + g
            after, before = (g + 1) % peers, (g + peers - 1) % peers
            water = density = None
            for kind in range(2):
                for t in range(tiles):
                    at = (kind * tiles + t) * sub
                    if kind == 0:
                        piece = spin(ends[t], at - g * sub)
                    else:
                        piece = jnp.where(early, spin(ends[t], at - after * sub), spin(ends[t], at - before * sub))
                    water = piece if water is None else jnp.where(lane >= at, piece, water)
            for t in range(tiles):
                piece = spin(surface[t], (t - e) * sub)
                density = piece if density is None else jnp.where(lane >= t * sub, piece, density)
            payload_ref[e, :TILE, :] = water
            payload_ref[e, TILE:, :] = density


def corner_kernel(got_ref, left_ref, right_ref, up_ref, down_ref, water_ref):
    half_lanes = LANES // 2
    lane = lane_index()
    groups = got_ref.shape[0]
    sub = LANES // groups
    height = water_ref.shape[1]
    tiles = height // TILE
    for kind in range(2):
        for t in range(tiles):
            rows = slice(TILE * t, TILE * (t + 1))
            value = None
            for c in range(groups):
                piece = spin(got_ref[c, :TILE, :], (c - kind * tiles - t) * sub)
                value = piece if value is None else jnp.where(lane >= c * sub, piece, value)
            water_ref[kind, rows, :] = value
            if TILE * t >= height - HALO:
                up_ref[DIRS + 1 + kind, TILE * t - height + HALO : TILE * (t + 1) - height + HALO, :] = value
            if TILE * t < HALO:
                down_ref[DIRS + 1 + kind, rows, :] = value
    for i in range(DIRS + 1):
        for t in range(HALO // TILE):
            rows = slice(TILE * t, TILE * (t + 1))
            left, right = left_ref[i, rows, :], right_ref[i, rows, :]
            up_ref[i, rows, :] = jnp.where(lane < half_lanes, spin(left, half_lanes), right)
            down_ref[i, rows, :] = jnp.where(lane < half_lanes, left, spin(right, half_lanes))


def sheet_kernel(got_ref, sheet_ref, current_ref, out_ref):
    groups = got_ref.shape[0]
    peers = groups // 2
    sub = LANES // groups
    cells, height, columns = sheet_ref.shape
    lane = lane_index()
    for t in range(height // TILE):
        rows = slice(TILE * t, TILE * (t + 1))
        inflow = []
        for which in range(2):
            rho = None
            for g in range(peers):
                piece = spin(got_ref[which * peers + g, TILE:, :], (g - t) * sub)
                rho = piece if rho is None else jnp.where(lane >= g * sub, piece, rho)
            end = sheet_ref[0 if which == 0 else cells - 1, rows, :]
            inflow.append(uptake_rate * (uptake(rho[:, :columns]) - end))
        drag = drag_rate * current_ref[rows, :]
        source = sheet_ref
        for _ in range(SUBSTEPS):
            below = source[0, rows, :]
            spread_below = base_diffusion + slope_diffusion * below
            entering = inflow[0]
            for k in range(cells):
                if k + 1 < cells:
                    above = source[k + 1, rows, :]
                    spread = base_diffusion + slope_diffusion * above
                    leaving = -0.5 * (spread + spread_below) * (above - below) + drag * below
                else:
                    above = spread = None
                    leaving = -inflow[1]
                out_ref[k, rows, :] = below + (entering - leaving)
                below, spread_below, entering = above, spread, leaving
            source = out_ref


def ring(axis, shift):
    count = lax.axis_size(axis)
    return [(i, (i + shift) % count) for i in range(count)]


def on_device(populations, solid_mask, water_sheet, current):
    lattice = populations[0]
    solids = solid_mask[0]
    layers, height, width = lattice.shape[1:]
    groups = lax.axis_size(("side", "gy"))
    f32 = jnp.float32
    mask_values = solids.astype(f32)[None]

    def shape(*dims):
        return jax.ShapeDtypeStruct(dims, f32)

    def rows_of(cut):
        return jnp.concatenate([lattice[:, :, cut], mask_values[:, :, cut]])

    low = lax.ppermute(rows_of(slice(height - HALO, height)), "gx", ring("gx", 1))
    high = lax.ppermute(rows_of(slice(0, HALO)), "gx", ring("gx", -1))

    ends = jnp.stack([water_sheet[0], water_sheet[-1]])
    ends = jnp.pad(ends, ((0, 0), (0, 0), (0, LANES - ends.shape[2])))
    me = lax.axis_index(("side", "gy")).reshape(1)
    strip = shape(DIRS + 1, height // 2, LANES)
    send_left, send_right, payload = pl.pallas_call(
        strip_kernel, out_shape=(strip, strip, shape(groups, 2 * TILE, LANES)),
        in_specs=[pl.BlockSpec(memory_space=pltpu.SMEM), VMEM, VMEM, VMEM], out_specs=(VMEM,) * 3,
        compiler_params=pltpu.CompilerParams(vmem_limit_bytes=8 << 20),
    )(me, lattice, solids, ends)
    left = lax.ppermute(send_right, "gy", ring("gy", 1))
    right = lax.ppermute(send_left, "gy", ring("gy", -1))
    got = lax.all_to_all(payload, ("side", "gy"), split_axis=0, concat_axis=0, tiled=True)

    corner = shape(DIRS + 3, HALO, LANES)
    send_up, send_down, water_here = pl.pallas_call(
        corner_kernel, out_shape=(corner, corner, shape(2, height, width)),
        in_specs=[VMEM] * 3, out_specs=(VMEM,) * 3,
        compiler_params=pltpu.CompilerParams(vmem_limit_bytes=8 << 20),
    )(got, left, right)
    corner_low = lax.ppermute(send_up, "gx", ring("gx", 1))
    corner_high = lax.ppermute(send_down, "gx", ring("gx", -1))
    water = pl.pallas_call(
        sheet_kernel, out_shape=shape(*water_sheet.shape),
        in_specs=[VMEM] * 3, out_specs=VMEM,
        compiler_params=pltpu.CompilerParams(vmem_limit_bytes=8 << 20),
    )(got, water_sheet, current)
    out = pl.pallas_call(
        lattice_kernel, out_shape=shape(*lattice.shape),
        in_specs=[VMEM] * 9, out_specs=VMEM,
        compiler_params=pltpu.CompilerParams(vmem_limit_bytes=36 << 20),
        scratch_shapes=window_scratch(layers, height + 2 * HALO),
        cost_estimate=pl.CostEstimate(flops=1 << 28, bytes_accessed=8 << 20, transcendentals=0),
    )(lattice, solids, water_here, low, high, left, right, corner_low, corner_high)
    return (out[None], water)


def solution(mesh):
    in_specs = (
        P("side", None, None, "gx", "gy"),
        P("side", None, "gx", "gy"),
        P(None, "gx", ("side", "gy")),
        P("gx", ("side", "gy")),
    )
    out_specs = (P("side", None, None, "gx", "gy"), P(None, "gx", ("side", "gy")))
    return jax.shard_map(
        on_device, mesh=mesh, in_specs=in_specs, out_specs=out_specs, check_vma=False
    )
```

time: 74.7 us -> 51.3 us (0.69)
  Pallas kernels: 38.6 us -> 24.2 us
  blocking collectives: 0 us -> 9.57 us
  waiting for transfers between devices: 11.2 us -> 3.89 us
  local copies, waits for them, and re-layouts: 6.34 us -> 1.43 us
  starting transfers between devices: 12.9 us -> 9.5 us
  other arithmetic: 4.34 us -> 1.8 us
    pallas_call x4, Pallas kernels: 38.6 us -> 24.2 us  [the longest x1 22.1 us: on_device(): pl.pallas_call(lattice_kernel, out_shape=shape(*lattice.shape), in_specs=...]
    all_to_all x0 -> x1, blocking collectives: none -> 9.57 us  [on_device(): lax.all_to_all(payload, ('side', 'gy'), split_axis=0, concat_axis=0, tile...]
    all_to_all x1 -> x0, starting transfers between devices: 6.37 us -> none  [on_device(): lax.all_to_all(payload, ('side', 'gy'), split_axis=0, concat_axis=0, tile...]
    ppermute x1, waiting for transfers between devices: 3.52 us -> 0.01 us  [on_device(): right = lax.ppermute(send_left, 'gy', ring('gy', -1))]
    unnamed x20 -> x8, local copies, waits for them, and re-layouts: 3.06 us -> 0.02 us
    ppermute x1, starting transfers between devices: 0.97 us -> 3.47 us  [on_device(): corner_low = lax.ppermute(send_up, 'gx', ring('gx', 1))]
    ppermute x1, waiting for transfers between devices: 2.35 us -> 0.01 us  [on_device(): left = lax.ppermute(send_right, 'gy', ring('gy', 1))]
    ppermute x1, waiting for transfers between devices: 3.33 us -> 1.53 us  [on_device(): corner_high = lax.ppermute(send_down, 'gx', ring('gx', -1))]
  transfers between devices with their start and end apart: 7 -> 6, of which waited for: 4 -> 2; matrix products, arithmetic and copies ran while one was open for 6% -> 2% of each run, Pallas kernels for 6% -> 4%
where the time goes in v2:
time: 51.3 us; the launch traced here: 51.1 us
  Pallas kernels  24.2 us (47%)
  blocking collectives  9.57 us (19%)
  starting transfers between devices  9.5 us (19%)
  waiting for transfers between devices  3.89 us (8%)
  other arithmetic  1.8 us (4%)
  local copies, waits for them, and re-layouts  1.43 us (3%)
  between operations  0.73 us (1%)
    pallas_call x1, Pallas kernels, on_device(): pl.pallas_call(lattice_kernel, out_shape=shape(*lattice.shape), in_specs=...  22.1 us
    all_to_all x1, blocking collectives, on_device(): lax.all_to_all(payload, ('side', 'gy'), split_axis=0, concat_axis=0, tile...  9.57 us
    ppermute x1, starting transfers between devices, on_device(): corner_low = lax.ppermute(send_up, 'gx', ring('gx', 1))  3.47 us
    ppermute x1, starting transfers between devices, on_device(): lax.ppermute(rows_of(slice(height - HALO, height)), 'gx', ring('gx', 1))  2.59 us
    ppermute x1, waiting for transfers between devices, on_device(): corner_low = lax.ppermute(send_up, 'gx', ring('gx', 1))  2.36 us
    ppermute x1, starting transfers between devices, on_device(): right = lax.ppermute(send_left, 'gy', ring('gy', -1))  2.09 us
    concatenate x2, other arithmetic, rows_of(): return jnp.concatenate([lattice[:, :, cut], mask_values[:, :, cut]])  1.79 us
    ppermute x1, waiting for transfers between devices, on_device(): corner_high = lax.ppermute(send_down, 'gx', ring('gx', -1))  1.53 us
  transfers between devices with their start and end apart: 6, of which 2 were waited for; matrix products, arithmetic and copies ran while one was open for 2% of the time, Pallas kernels for 4%

profile of v2, /device:TPU:1, one launch (start us, length us, event | category | flops | bytes accessed | tf_op | source)
XLA Modules:
  0.0 51.1 jit_solution(16921233559505025501)
XLA Ops:
  0.6 0.0 copy-start.2
  0.6 1.4 %fusion = (f32[19,4,16,128]{3,2,1,0:T(8,128)S(1)}, f32[19,4,16,128]{3,2,1,0:T(8,128)S(1)}) fusion(f32[19,4,32,128]{3,2,1,0:T(8,128)} %bitcast.4), kind=kLoop, calls=%fused_computation.4 | loop fusion | bytes 2490368 | tf_op jit(solution)/shard_map/slice | solution.py:465
  2.0 0.0 copy-done.2
  2.1 0.0 copy-start.1
  2.1 0.0 copy-start
  2.1 0.9 %pad_maximum_fusion = f32[20,4,16,128]{3,2,1,0:T(8,128)} fusion(f32[1,4,16,128]{3,2,1,0:T(8,128)S(1)} %get-tuple-element.19, f32[19,4,16,128]{3,2,1,0:T(8,128)S(1)} %get-tuple-element.15), kind=kLoop, calls=%fused_computation | loop fusion | flops 163840 | bytes 1310720 | tf_op jit(solution)/shard_map/concatenate | solution.py:465
  3.0 2.6 %collective-permute-start.2 = (f32[20,4,16,128]{3,2,1,0:T(8,128)}, f32[20,4,16,128]{3,2,1,0:T(8,128)S(1)}, u32[]{:S(2)}, u32[]{:S(2)}) collective-permute-start(f32[20,4,16,128]{3,2,1,0:T(8,128)} %pad_maximum_fusion), channel_id=1, source_target_pairs={{0,4},{4,8},{8,12},{12,0},{1,5},{5,9},{9,13},{13,1},{2,6},{6,10},{... | collective-permute-start | bytes 1966088 | tf_op jit(solution)/shard_map/ppermute | solution.py:467
  5.6 0.9 %pad_maximum_fusion.1 = f32[20,4,16,128]{3,2,1,0:T(8,128)} fusion(f32[1,4,16,128]{3,2,1,0:T(8,128)S(1)} %get-tuple-element.18, f32[19,4,16,128]{3,2,1,0:T(8,128)S(1)} %get-tuple-element.14), kind=kLoop, calls=%fused_computation.1 | loop fusion | flops 163840 | bytes 1310720 | tf_op jit(solution)/shard_map/concatenate | solution.py:465
  6.5 0.0 copy-start.3
  6.5 0.0 collective-permute-start.3
  6.5 0.0 copy-done.1
  6.5 0.0 copy-done
  6.5 0.7 %shard_map.59 = (f32[20,16,128]{2,1,0:T(8,128)S(1)}, f32[20,16,128]{2,1,0:T(8,128)S(1)}, f32[8,16,128]{2,1,0:T(8,128)S(1)}) custom-call(s32[1]{0:T(128)} %bitcast.2.me_ref, f32[19,4,32,128]{3,2,1,0:T(8,128)S(1)} %bitcast.5, s32[4,32,128]{2,1,0:T(8,128)S(1)} %bitcast.7, f32[2,32,128]{2,1,0:T(8,128)S(1)} %select_maximum_fusion.ends_ref), custom_call_target="tpu_custom_call" | custom-call | tf_op jit(solution)/shard_map/pallas_call | solution.py:474
  7.3 1.3 %collective-permute-start = (f32[20,16,128]{2,1,0:T(8,128)S(1)}, f32[20,16,128]{2,1,0:T(8,128)S(1)}, u32[]{:S(2)}, u32[]{:S(2)}) collective-permute-start(f32[20,16,128]{2,1,0:T(8,128)S(1)} %get-tuple-element.9), channel_id=1, source_target_pairs={{0,1},{1,2},{2,3},{3,0},{4,5},{5,6},{6,7},{7,4},{8,9},{9,10},{10,1... | collective-permute-start | bytes 491528 | tf_op jit(solution)/shard_map/ppermute | solution.py:479
  8.6 2.1 %collective-permute-start.1 = (f32[20,16,128]{2,1,0:T(8,128)S(1)}, f32[20,16,128]{2,1,0:T(8,128)S(1)}, u32[]{:S(2)}, u32[]{:S(2)}) collective-permute-start(f32[20,16,128]{2,1,0:T(8,128)S(1)} %get-tuple-element.10), channel_id=1, source_target_pairs={{0,3},{1,0},{2,1},{3,2},{4,7},{5,4},{6,5},{7,6},{8,11},{9,8},{10,9... | collective-permute-start | bytes 491528 | tf_op jit(solution)/shard_map/ppermute | solution.py:480
  10.7 9.6 %all_to_all.5.got_ref = f32[8,16,128]{2,1,0:T(8,128)S(1)} all-to-all(f32[8,16,128]{2,1,0:T(8,128)S(1)} %get-tuple-element.8), channel_id=1, replica_groups=mesh['side'=2,'gx'=4,'gy'=4] {'side','gy'}, dimensions={0} | all-to-all | bytes 131072 | tf_op jit(solution)/shard_map/all_to_all | solution.py:481
  20.3 0.0 collective-permute-done.left_ref
  20.3 0.0 collective-permute-done.1.right_ref
  20.3 0.2 shard_map.60
  20.5 3.5 %collective-permute-start.4 = (f32[22,16,128]{2,1,0:T(8,128)S(1)}, f32[22,16,128]{2,1,0:T(8,128)S(1)}, u32[]{:S(2)}, u32[]{:S(2)}) collective-permute-start(f32[22,16,128]{2,1,0:T(8,128)S(1)} %get-tuple-element.12), channel_id=1, source_target_pairs={{0,4},{4,8},{8,12},{12,0},{1,5},{5,9},{9,13},{13,1},{2,6},{6,10},{... | collective-permute-start | bytes 540680 | tf_op jit(solution)/shard_map/ppermute | solution.py:489
  24.0 0.0 collective-permute-start.5
  24.0 0.0 copy-done.3
  24.0 1.2 %shard_map.62 = f32[32,32,64]{2,1,0:T(8,128)} custom-call(f32[8,16,128]{2,1,0:T(8,128)S(1)} %all_to_all.5.got_ref, f32[32,32,64]{2,1,0:T(8,128)S(1)} %copy-done.1, f32[32,64]{1,0:T(8,128)S(1)} %copy-done.3), custom_call_target="tpu_custom_call" | custom-call | tf_op jit(solution)/shard_map/pallas_call | solution.py:491
  25.2 2.4 %collective-permute-done.4.clow_ref = f32[22,16,128]{2,1,0:T(8,128)S(1)} collective-permute-done((f32[22,16,128]{2,1,0:T(8,128)S(1)}, f32[22,16,128]{2,1,0:T(8,128)S(1)}, u32[]{:S(2)}, u32[]{:S(2)}) %collective-permute-start.4) | collective-permute-done | bytes 180256 | tf_op jit(solution)/shard_map/ppermute | solution.py:489
  27.5 1.5 %collective-permute-done.5.chigh_ref = f32[22,16,128]{2,1,0:T(8,128)S(1)} collective-permute-done((f32[22,16,128]{2,1,0:T(8,128)S(1)}, f32[22,16,128]{2,1,0:T(8,128)S(1)}, u32[]{:S(2)}, u32[]{:S(2)}) %collective-permute-start.5) | collective-permute-done | bytes 180256 | tf_op jit(solution)/shard_map/ppermute | solution.py:490
  29.1 0.0 collective-permute-done.2.low_ref
  29.1 0.0 collective-permute-done.3.high_ref
  29.1 22.1 %shard_map.61 = f32[19,4,32,128]{3,2,1,0:T(8,128)} custom-call(f32[19,4,32,128]{3,2,1,0:T(8,128)S(1)} %bitcast.6, s32[4,32,128]{2,1,0:T(8,128)S(1)} %bitcast.8, f32[2,32,128]{2,1,0:T(8,128)S(1)} %get-tuple-element.11.water_ref, f32[20,4,16,128]{3,2,1,0:T(8,128)S(1)} %collective-permute-done.2.low_ref, ...), custom_call_target="tpu_custom_call" | custom-call | flops 268435456 | bytes 8388608 | tf_op jit(solution)/shard_map/pallas_call | solution.py:496
  (4 shorter events, 0.0 us)
Async XLA Ops:
  0.6 1.4 %copy-start.2 = (s32[1,4,32,128]{3,2,1,0:T(8,128)S(1)}, s32[1,4,32,128]{3,2,1,0:T(8,128)}, u32[]{:S(2)}) copy-start(s32[1,4,32,128]{3,2,1,0:T(8,128)} %param.5) | copy-start | bytes 196612
  2.1 4.4 %copy-start.1 = (f32[32,32,64]{2,1,0:T(8,128)S(1)}, f32[32,32,64]{2,1,0:T(8,128)}, u32[]{:S(2)}) copy-start(f32[32,32,64]{2,1,0:T(8,128)} %sheet_ref.1) | copy-start | bytes 786436
  2.1 4.4 %copy-start = (f32[1,19,4,32,128]{4,3,2,1,0:T(8,128)S(1)}, f32[1,19,4,32,128]{4,3,2,1,0:T(8,128)}, u32[]{:S(2)}) copy-start(f32[1,19,4,32,128]{4,3,2,1,0:T(8,128)} %param.4) | copy-start | bytes 3735556
  3.0 26.1 %collective-permute-start.2 = (f32[20,4,16,128]{3,2,1,0:T(8,128)}, f32[20,4,16,128]{3,2,1,0:T(8,128)S(1)}, u32[]{:S(2)}, u32[]{:S(2)}) collective-permute-start(f32[20,4,16,128]{3,2,1,0:T(8,128)} %pad_maximum_fusion), channel_id=1, source_target_pairs={{0,4},{4,8},{8,12},{12,0},{1,5},{5,9},{9,13},{13,1},{2,6},{6,10},{... | collective-permute-start | bytes 1966088 | tf_op jit(solution)/shard_map/ppermute | solution.py:467
  6.5 17.5 %copy-start.3 = (f32[32,64]{1,0:T(8,128)S(1)}, f32[32,64]{1,0:T(8,128)}, u32[]{:S(2)}) copy-start(f32[32,64]{1,0:T(8,128)} %current_ref.1) | copy-start | bytes 24580
  6.5 22.6 %collective-permute-start.3 = (f32[20,4,16,128]{3,2,1,0:T(8,128)}, f32[20,4,16,128]{3,2,1,0:T(8,128)S(1)}, u32[]{:S(2)}, u32[]{:S(2)}) collective-permute-start(f32[20,4,16,128]{3,2,1,0:T(8,128)} %pad_maximum_fusion.1), channel_id=1, source_target_pairs={{0,12},{4,0},{8,4},{12,8},{1,13},{5,1},{9,5},{13,9},{2,14},{6,2},{... | collective-permute-start | bytes 1966088 | tf_op jit(solution)/shard_map/ppermute | solution.py:468
  7.3 13.0 %collective-permute-start = (f32[20,16,128]{2,1,0:T(8,128)S(1)}, f32[20,16,128]{2,1,0:T(8,128)S(1)}, u32[]{:S(2)}, u32[]{:S(2)}) collective-permute-start(f32[20,16,128]{2,1,0:T(8,128)S(1)} %get-tuple-element.9), channel_id=1, source_target_pairs={{0,1},{1,2},{2,3},{3,0},{4,5},{5,6},{6,7},{7,4},{8,9},{9,10},{10,1... | collective-permute-start | bytes 491528 | tf_op jit(solution)/shard_map/ppermute | solution.py:479
  8.6 11.7 %collective-permute-start.1 = (f32[20,16,128]{2,1,0:T(8,128)S(1)}, f32[20,16,128]{2,1,0:T(8,128)S(1)}, u32[]{:S(2)}, u32[]{:S(2)}) collective-permute-start(f32[20,16,128]{2,1,0:T(8,128)S(1)} %get-tuple-element.10), channel_id=1, source_target_pairs={{0,3},{1,0},{2,1},{3,2},{4,7},{5,4},{6,5},{7,6},{8,11},{9,8},{10,9... | collective-permute-start | bytes 491528 | tf_op jit(solution)/shard_map/ppermute | solution.py:480
  20.5 7.0 %collective-permute-start.4 = (f32[22,16,128]{2,1,0:T(8,128)S(1)}, f32[22,16,128]{2,1,0:T(8,128)S(1)}, u32[]{:S(2)}, u32[]{:S(2)}) collective-permute-start(f32[22,16,128]{2,1,0:T(8,128)S(1)} %get-tuple-element.12), channel_id=1, source_target_pairs={{0,4},{4,8},{8,12},{12,0},{1,5},{5,9},{9,13},{13,1},{2,6},{6,10},{... | collective-permute-start | bytes 540680 | tf_op jit(solution)/shard_map/ppermute | solution.py:489
  24.0 5.1 %collective-permute-start.5 = (f32[22,16,128]{2,1,0:T(8,128)S(1)}, f32[22,16,128]{2,1,0:T(8,128)S(1)}, u32[]{:S(2)}, u32[]{:S(2)}) collective-permute-start(f32[22,16,128]{2,1,0:T(8,128)S(1)} %get-tuple-element.13), channel_id=1, source_target_pairs={{0,12},{4,0},{8,4},{12,8},{1,13},{5,1},{9,5},{13,9},{2,14},{6,2},{... | collective-permute-start | bytes 540680 | tf_op jit(solution)/shard_map/ppermute | solution.py:490

commit v3 on v2

--- a/solution.py
+++ b/solution.py
@@ -10,6 +10,7 @@
 SUBSTEPS = 2
 HALO = 2 * STEPS
 TILE = 8
+FRONT = TILE
 LANES = 128
 WINDOWS = 2
 
@@ -40,7 +41,6 @@
 drag_rate = 0.03
 base_diffusion = 0.05
 slope_diffusion = 0.015
-ROOT2 = 2.0**0.5
 
 VMEM = pl.BlockSpec(memory_space=pltpu.VMEM)
 
@@ -77,14 +77,12 @@
         )
     rho = rho + partial[0]
     density_ref[z, rows, :] = rho
-    psi_ref[z, rows, :] = jnp.where(pore > 0.5, 1.0 - jnp.exp(-rho), wall_potential)
+    psi_ref[z, rows, :] = jnp.where(pore > 0.0, 1.0 - jnp.exp(-rho), wall_potential)
     return rho
 
 
 def run_steps(refs, layers, window_rows):
-    (posts, sets, pull_ref, pore_ref, flux_ref) = refs
-    spare = window_rows + 2 * TILE
-    planes = [(w * layers, w * layers + z, z) for w in range(WINDOWS) for z in range(layers)]
+    planes = [(0, z, z) for z in range(layers)]
 
     def across(values, base, z, sign):
         above = values[base + z + 1] if z + 1 < layers else None
@@ -97,8 +95,11 @@
             return above
         return above + below if sign > 0 else above - below
 
-    def gather(row, target):
-        even_ref, odd_ref, density_ref, psi_ref = target
+    def gather(row, window, parity):
+        row = row + FRONT
+        posts, sets, share_ref = refs[window][:3]
+        target = sets[parity]
+        even_ref, odd_ref, density_ref, psi_ref = target[:4]
         rows = pl.ds(row, TILE)
         for base, p, z in planes:
             values = []
@@ -106,36 +107,42 @@
                 _, shift_y, shift_z = velocity_table[i]
                 reflected = z - shift_z < 0 or z - shift_z >= layers
                 values.append(spin(posts[i, p, rows, :], 0 if reflected else shift_y))
-            set_pairs(values, row, p, even_ref, odd_ref, None, density_ref, psi_ref, pore_ref[p, rows, :])
-
-    def pull(row, source):
-        psi_ref = source[3]
-        rows = pl.ds(row, TILE)
-        centre = [psi_ref[p, rows, :] for _, p, _ in planes]
-        plus = [psi_ref[p, pl.ds(row + 1, TILE), :] for _, p, _ in planes]
-        minus = [psi_ref[p, pl.ds(row - 1, TILE), :] for _, p, _ in planes]
-        slope = [a - b for a, b in zip(plus, minus)]
-        pair = [a + b for a, b in zip(plus, minus)]
-        for base, p, z in planes:
-            lift = across(centre, base, z, -1)
-            shell = (centre[p] + centre[p]) + pair[p] + across(centre, base, z, 1)
-            pull_ref[0, p, rows, :] = (
-                (slope[p] + slope[p]) + across(slope, base, z, 1) + (spin(slope[p], 1) + spin(slope[p], -1))
-            )
-            pull_ref[1, p, rows, :] = spin(shell, -1) - spin(shell, 1)
-            pull_ref[2, p, rows, :] = (
-                (lift + lift) + across(pair, base, z, -1) + (spin(lift, 1) + spin(lift, -1))
-            )
-
-    def collide(row, source):
-        even_ref, odd_ref, density_ref, psi_ref = source
+            set_pairs(values, row, p, even_ref, odd_ref, None, density_ref, psi_ref, share_ref[p, rows, :])
+
+    def fold(row, window, parity):
+        row = row + FRONT
+        _, _, _, psi_ref, around_ref, tilt_ref = refs[window][1][parity]
         rows = pl.ds(row, TILE)
         for base, p, z in planes:
+            centre = psi_ref[p, rows, :]
+            left, right = spin(centre, 1), spin(centre, -1)
+            around_ref[p, rows, :] = (centre + centre) + (left + right)
+            tilt_ref[p, rows, :] = right - left
+
+    def collide(row, window, parity):
+        row = row + FRONT
+        posts, sets, share_ref, even_keep_ref, odd_keep_ref, flux_ref = refs[window]
+        even_ref, odd_ref, density_ref, psi_ref, around_ref, tilt_ref = sets[parity]
+        rows, up, down = (pl.ds(row + shift, TILE) for shift in (0, 1, -1))
+        slope, column, tilt = {}, {}, {}
+        for base, p, z in planes:
+            for q in range(max(base, p - 1), min(base + layers, p + 2)):
+                if q not in slope:
+                    plus, minus = psi_ref[q, up, :], psi_ref[q, down, :]
+                    slope[q] = plus - minus
+                    column[q] = (plus + minus) + around_ref[q, rows, :]
+                    tilt[q] = tilt_ref[q, rows, :]
+            pulls = (
+                (around_ref[p, up, :] - around_ref[p, down, :]) + across(slope, base, z, 1),
+                ((tilt[p] + tilt[p]) + (tilt_ref[p, up, :] + tilt_ref[p, down, :]))
+                + across(tilt, base, z, 1),
+                across(column, base, z, -1),
+            )
             rho = density_ref[p, rows, :]
-            is_pore = pore_ref[p, rows, :] > 0.5
             delta = [None] + [odd_ref[k, p, rows, :] for k in range(9)]
             pulled = psi_ref[p, rows, :] * (1.0 / 15.0)
-            scale = jnp.where(is_pore, (3.0 / ROOT2) / rho, 0.0)
+            a_diag = rho * share_ref[p, rows, :]
+            scale = jnp.where(share_ref[p, rows, :] > 0.0, 1.5 / rho, 0.0)
             u = []
             for component in range(3):
                 value = None
@@ -146,15 +153,14 @@
                             value = delta[k]
                         else:
                             value = value + delta[k] if factor > 0 else value - delta[k]
-                u.append((value + pulled * pull_ref[component, p, rows, :]) * scale)
-            base = 1.0 - (u[0] * u[0] + u[1] * u[1] + u[2] * u[2]) * (1.0 / 3.0)
-            a_diag = jnp.where(is_pore, rho * (1.25 / 36.0), 0.0)
-            a_axis = a_diag + a_diag
-            o_diag = a_diag * ROOT2
-            o_axis = a_axis * ROOT2
-            keep_even = jnp.where(is_pore, -0.125, 0.5)
-            keep_odd = jnp.where(is_pore, -0.125, -0.5)
-            posts[0, p, rows, :] = posts[0, p, rows, :] * (keep_even + keep_even) + base * (a_diag * 12.0)
+                u.append((value + pulled * pulls[component]) * scale)
+            b_diag = a_diag - a_diag * ((u[0] * u[0] + u[1] * u[1] + u[2] * u[2]) * (2.0 / 3.0))
+            b_axis = b_diag + b_diag
+            o_diag = a_diag + a_diag
+            o_axis = o_diag + o_diag
+            keep_even = even_keep_ref[p, rows, :]
+            keep_odd = odd_keep_ref[p, rows, :]
+            posts[0, p, rows, :] = posts[0, p, rows, :] * (keep_even + keep_even) + b_diag * 12.0
             for k in range(1, 10):
                 i = 2 * k - 1
                 e = velocity_table[i]
@@ -169,15 +175,14 @@
                     else:
                         along = along - u[component]
                 axis = k <= 3
-                even = even_ref[k - 1, p, rows, :] * keep_even + (along * along + base) * (
-                    a_axis if axis else a_diag
-                )
-                odd = delta[k] * keep_odd + along * (o_axis if axis else o_diag)
+                drift = along * (o_axis if axis else o_diag)
+                even = (even_ref[k - 1, p, rows, :] * keep_even + (b_axis if axis else b_diag)) + drift * along
+                odd = delta[k] * keep_odd + drift
                 for j, sign, post in ((i, 1, even + odd), (i + 1, -1, even - odd)):
                     other = i + 1 if j == i else i
                     shift_x, _, shift_z = (sign * v for v in e)
                     if z + shift_z < 0:
-                        inflow = flux_ref[p // layers, rows, :] * (1.0 / 3.0 if axis else 1.0 / 6.0)
+                        inflow = flux_ref[rows, :] * (1.0 / 3.0 if axis else 1.0 / 6.0)
                         posts[other, p, rows, :] = post - inflow
                     elif z + shift_z >= layers:
                         posts[other, p, rows, :] = post
@@ -187,55 +192,73 @@
     def tiles_of(step):
         return (window_rows - 2 - 4 * step + TILE - 1) // TILE
 
-    def two_steps(pair, carry):
-        for half in range(2):
-            step = 2 * pair + half
-            first = 2 * step + 1
-            here, there = sets[half], sets[1 - half]
-            before = step - 1
-            last = jnp.where(step == 0, spare, 2 * before + TILE * (tiles_of(before) - 1))
-            gather(last, here)
-            pull(first, here)
-            pull(first + TILE, here)
-            collide(first, here)
-
-            def turn(tile, inner, first=first, here=here, there=there):
-                row = first + TILE * tile
-                pull(row + TILE, here)
-                gather(row - 1 - TILE, there)
-                collide(row, here)
-                return inner
-
-            lax.fori_loop(1, tiles_of(step), turn, 0)
-        return carry
-
-    lax.fori_loop(0, STEPS // 2, two_steps, 0)
-    gather(2 * (STEPS - 1) + TILE * (tiles_of(STEPS - 1) - 1), sets[STEPS % 2])
+    for step in range(STEPS):
+        half = step % 2
+        first = 2 * step + 1
+        if step:
+            last = 2 * (step - 1) + TILE * (tiles_of(step - 1) - 1)
+            for window in range(WINDOWS):
+                collide(first, window, half)
+            for window in range(WINDOWS):
+                fold(last - TILE, window, half)
+                gather(last, window, half)
+                fold(last, window, half)
+        else:
+            for window in range(WINDOWS):
+                collide(first, window, half)
+
+        def turn(tile, carry, first=first, half=half):
+            row = TILE * tile + first
+            gather(row - 1 - TILE, 0, 1 - half)
+            gather(row - 1 - TILE, 1, 1 - half)
+            collide(row, 0, half)
+            collide(row, 1, half)
+            fold(row - 1 - 2 * TILE, 0, 1 - half)
+            fold(row - 1 - 2 * TILE, 1, 1 - half)
+            return carry
+
+        lax.fori_loop(1, tiles_of(step), turn, 0)
+    for window in range(WINDOWS):
+        gather(2 * (STEPS - 1) + TILE * (tiles_of(STEPS - 1) - 1), window, STEPS % 2)
+
+
+def first_folds(refs, layers, window_rows):
+    for tile in range(window_rows // TILE):
+        rows = slice(FRONT + TILE * tile, FRONT + TILE * (tile + 1))
+        for window in range(WINDOWS):
+            psi_ref, around_ref, tilt_ref = refs[window][1][0][3:6]
+            for z in range(layers):
+                centre = psi_ref[z, rows, :]
+                left, right = spin(centre, 1), spin(centre, -1)
+                around_ref[z, rows, :] = (centre + centre) + (left + right)
+                tilt_ref[z, rows, :] = right - left
 
 
 def begin(read, read_pore, row, window, layers, refs):
-    (posts, sets, _, pore_ref, flux_ref) = refs
-    even_ref, odd_ref, density_ref, psi_ref = sets[0]
+    posts, sets, share_ref, even_keep_ref, odd_keep_ref, flux_ref = refs[window]
+    even_ref, odd_ref, density_ref, psi_ref = sets[0][:4]
+    row = row + FRONT
     rows = pl.ds(row, TILE)
     for z in range(layers):
-        p = window * layers + z
+        p = z
         pore = read_pore(z)
-        pore_ref[p, rows, :] = pore
+        is_pore = pore > 0.5
+        share_ref[p, rows, :] = jnp.where(is_pore, 1.25 / 36.0, 0.0)
+        even_keep_ref[p, rows, :] = jnp.where(is_pore, -0.125, 0.5)
+        odd_keep_ref[p, rows, :] = jnp.where(is_pore, -0.125, -0.5)
         values = [read(i, z) for i in range(DIRS)]
         rho = set_pairs(values, row, p, even_ref, odd_ref, posts.at[0], density_ref, psi_ref, pore)
         if z == 0:
-            flux_ref[window, rows, :] = uptake_rate * (uptake(rho) - flux_ref[window, rows, :])
+            flux_ref[rows, :] = uptake_rate * (uptake(rho) - flux_ref[rows, :])
 
 
 def finish(out_ref, refs, layers, height):
-    (posts, sets, _, _, _) = refs
-    even_ref, odd_ref = sets[STEPS % 2][:2]
     lane = lane_index()
     inside = (lane >= HALO) & (lane < LANES - HALO)
     move = 3 * HALO
 
     def tile_out(t, carry):
-        rows = pl.ds(HALO + TILE * t, TILE)
+        rows = pl.ds(FRONT + HALO + TILE * t, TILE)
         to = pl.ds(pl.multiple_of(TILE * t, TILE), TILE)
 
         def join(read):
@@ -244,10 +267,10 @@
             return jnp.where(inside, middle, edge)
 
         for z in range(layers):
-            out_ref[0, z, to, :] = join(lambda w: posts[0, w * layers + z, rows, :])
+            out_ref[0, z, to, :] = join(lambda w: refs[w][0][0, z, rows, :])
             for k in range(9):
-                even = join(lambda w: even_ref[k, w * layers + z, rows, :]) * 0.5
-                odd = join(lambda w: odd_ref[k, w * layers + z, rows, :]) * 0.5
+                even = join(lambda w: refs[w][1][STEPS % 2][0][k, z, rows, :]) * 0.5
+                odd = join(lambda w: refs[w][1][STEPS % 2][1][k, z, rows, :]) * 0.5
                 out_ref[2 * k + 1, z, to, :] = even + odd
                 out_ref[2 * k + 2, z, to, :] = even - odd
         return carry
@@ -256,20 +279,24 @@
 
 
 def window_scratch(layers, rows):
-    padded = rows + 3 * TILE
-    planes = WINDOWS * layers
+    padded = FRONT + rows + 2 * TILE
 
     def one(*lead):
         return pltpu.VMEM(lead + (padded, LANES), jnp.float32)
 
-    state = [one(9, planes), one(9, planes), one(planes), one(planes)]
-    return [one(DIRS, planes)] + state + state + [one(3, planes), one(planes), one(WINDOWS)]
+    state = [one(9, layers), one(9, layers)] + [one(layers)] * 4
+    return ([one(DIRS, layers)] + state + state + [one(layers)] * 3 + [one()]) * WINDOWS
+
+
+def window_refs(scratch):
+    count = len(scratch) // WINDOWS
+    parts = [scratch[count * w : count * (w + 1)] for w in range(WINDOWS)]
+    return [(part[0], (part[1:7], part[7:13])) + tuple(part[13:]) for part in parts]
 
 
 def lattice_kernel(f_ref, mask_ref, water_ref, low_ref, high_ref, left_ref, right_ref, clow_ref,
                    chigh_ref, out_ref, *scratch):
-    posts, e0, o0, d0, p0, e1, o1, d1, p1, pull_ref, pore_ref, flux_ref = scratch
-    refs = posts, ((e0, o0, d0, p0), (e1, o1, d1, p1)), pull_ref, pore_ref, flux_ref
+    refs = window_refs(scratch)
     layers, height = f_ref.shape[1], f_ref.shape[2]
     lane = lane_index()
     move = 3 * HALO
@@ -317,10 +344,11 @@
         def edge_of(i, z, own_of=own_of, halo=halo):
             return join(own_of(i, z), *halo(i, z))
 
-        flux_ref[0, TILE * tile : TILE * (tile + 1), :] = own
-        flux_ref[1, TILE * tile : TILE * (tile + 1), :] = join(own, spin(extra, move), extra)
+        refs[0][5][FRONT + TILE * tile : FRONT + TILE * (tile + 1), :] = own
+        refs[1][5][FRONT + TILE * tile : FRONT + TILE * (tile + 1), :] = join(own, spin(extra, move), extra)
         begin(own_of, lambda z, f=own_of: f(DIRS, z), TILE * tile, 0, layers, refs)
         begin(edge_of, lambda z, f=edge_of: f(DIRS, z), TILE * tile, 1, layers, refs)
+    first_folds(refs, layers, height + 2 * HALO)
     run_steps(refs, layers, height + 2 * HALO)
     finish(out_ref, refs, layers, height)
 

time: 51.3 us -> 47 us (0.916)
  Pallas kernels: 24.2 us -> 19.9 us
    pallas_call x1, Pallas kernels: 22.1 us -> 17.7 us  [on_device(): pl.pallas_call(lattice_kernel, out_shape=shape(*lattice.shape), in_specs=...]
  transfers between devices with their start and end apart: 6 -> 6, of which waited for: 2 -> 2; matrix products, arithmetic and copies ran while one was open for 2% -> 2% of each run, Pallas kernels for 4% -> 5%
where the time goes in v3:
time: 47 us; the launch traced here: 46.8 us
  Pallas kernels  19.9 us (42%)
  blocking collectives  9.57 us (20%)
  starting transfers between devices  9.5 us (20%)
  waiting for transfers between devices  3.89 us (8%)
  other arithmetic  1.8 us (4%)
  local copies, waits for them, and re-layouts  1.43 us (3%)
  between operations  0.73 us (2%)
    pallas_call x1, Pallas kernels, on_device(): pl.pallas_call(lattice_kernel, out_shape=shape(*lattice.shape), in_specs=...  17.7 us
    all_to_all x1, blocking collectives, on_device(): lax.all_to_all(payload, ('side', 'gy'), split_axis=0, concat_axis=0, tile...  9.57 us
    ppermute x1, starting transfers between devices, on_device(): corner_low = lax.ppermute(send_up, 'gx', ring('gx', 1))  3.47 us
    ppermute x1, starting transfers between devices, on_device(): lax.ppermute(rows_of(slice(height - HALO, height)), 'gx', ring('gx', 1))  2.59 us
    ppermute x1, waiting for transfers between devices, on_device(): corner_low = lax.ppermute(send_up, 'gx', ring('gx', 1))  2.36 us
    ppermute x1, starting transfers between devices, on_device(): right = lax.ppermute(send_left, 'gy', ring('gy', -1))  2.09 us
    concatenate x2, other arithmetic, rows_of(): return jnp.concatenate([lattice[:, :, cut], mask_values[:, :, cut]])  1.79 us
    ppermute x1, waiting for transfers between devices, on_device(): corner_high = lax.ppermute(send_down, 'gx', ring('gx', -1))  1.53 us
  transfers between devices with their start and end apart: 6, of which 2 were waited for; matrix products, arithmetic and copies ran while one was open for 2% of the time, Pallas kernels for 5%

profile of v3, /device:TPU:1, one launch (start us, length us, event | category | flops | bytes accessed | tf_op | source)
XLA Modules:
  0.0 46.8 jit_solution(14309410374968170360)
XLA Ops:
  0.6 0.0 copy-start.2
  0.6 1.4 %fusion = (f32[19,4,16,128]{3,2,1,0:T(8,128)S(1)}, f32[19,4,16,128]{3,2,1,0:T(8,128)S(1)}) fusion(f32[19,4,32,128]{3,2,1,0:T(8,128)} %bitcast.4), kind=kLoop, calls=%fused_computation.4 | loop fusion | bytes 2490368 | tf_op jit(solution)/shard_map/slice | solution.py:493
  2.0 0.0 copy-done.2
  2.1 0.0 copy-start.1
  2.1 0.0 copy-start
  2.1 0.9 %pad_maximum_fusion = f32[20,4,16,128]{3,2,1,0:T(8,128)} fusion(f32[1,4,16,128]{3,2,1,0:T(8,128)S(1)} %get-tuple-element.19, f32[19,4,16,128]{3,2,1,0:T(8,128)S(1)} %get-tuple-element.15), kind=kLoop, calls=%fused_computation | loop fusion | flops 163840 | bytes 1310720 | tf_op jit(solution)/shard_map/concatenate | solution.py:493
  3.0 2.6 %collective-permute-start.2 = (f32[20,4,16,128]{3,2,1,0:T(8,128)}, f32[20,4,16,128]{3,2,1,0:T(8,128)S(1)}, u32[]{:S(2)}, u32[]{:S(2)}) collective-permute-start(f32[20,4,16,128]{3,2,1,0:T(8,128)} %pad_maximum_fusion), channel_id=1, source_target_pairs={{0,4},{4,8},{8,12},{12,0},{1,5},{5,9},{9,13},{13,1},{2,6},{6,10},{... | collective-permute-start | bytes 1966088 | tf_op jit(solution)/shard_map/ppermute | solution.py:495
  5.6 0.9 %pad_maximum_fusion.1 = f32[20,4,16,128]{3,2,1,0:T(8,128)} fusion(f32[1,4,16,128]{3,2,1,0:T(8,128)S(1)} %get-tuple-element.18, f32[19,4,16,128]{3,2,1,0:T(8,128)S(1)} %get-tuple-element.14), kind=kLoop, calls=%fused_computation.1 | loop fusion | flops 163840 | bytes 1310720 | tf_op jit(solution)/shard_map/concatenate | solution.py:493
  6.5 0.0 copy-start.3
  6.5 0.0 collective-permute-start.3
  6.5 0.0 copy-done.1
  6.5 0.0 copy-done
  6.5 0.7 %shard_map.59 = (f32[20,16,128]{2,1,0:T(8,128)S(1)}, f32[20,16,128]{2,1,0:T(8,128)S(1)}, f32[8,16,128]{2,1,0:T(8,128)S(1)}) custom-call(s32[1]{0:T(128)} %bitcast.2.me_ref, f32[19,4,32,128]{3,2,1,0:T(8,128)S(1)} %bitcast.5, s32[4,32,128]{2,1,0:T(8,128)S(1)} %bitcast.7, f32[2,32,128]{2,1,0:T(8,128)S(1)} %select_maximum_fusion.ends_ref), custom_call_target="tpu_custom_call" | custom-call | tf_op jit(solution)/shard_map/pallas_call | solution.py:502
  7.3 1.3 %collective-permute-start = (f32[20,16,128]{2,1,0:T(8,128)S(1)}, f32[20,16,128]{2,1,0:T(8,128)S(1)}, u32[]{:S(2)}, u32[]{:S(2)}) collective-permute-start(f32[20,16,128]{2,1,0:T(8,128)S(1)} %get-tuple-element.9), channel_id=1, source_target_pairs={{0,1},{1,2},{2,3},{3,0},{4,5},{5,6},{6,7},{7,4},{8,9},{9,10},{10,1... | collective-permute-start | bytes 491528 | tf_op jit(solution)/shard_map/ppermute | solution.py:507
  8.6 2.1 %collective-permute-start.1 = (f32[20,16,128]{2,1,0:T(8,128)S(1)}, f32[20,16,128]{2,1,0:T(8,128)S(1)}, u32[]{:S(2)}, u32[]{:S(2)}) collective-permute-start(f32[20,16,128]{2,1,0:T(8,128)S(1)} %get-tuple-element.10), channel_id=1, source_target_pairs={{0,3},{1,0},{2,1},{3,2},{4,7},{5,4},{6,5},{7,6},{8,11},{9,8},{10,9... | collective-permute-start | bytes 491528 | tf_op jit(solution)/shard_map/ppermute | solution.py:508
  10.7 9.6 %all_to_all.5.got_ref = f32[8,16,128]{2,1,0:T(8,128)S(1)} all-to-all(f32[8,16,128]{2,1,0:T(8,128)S(1)} %get-tuple-element.8), channel_id=1, replica_groups=mesh['side'=2,'gx'=4,'gy'=4] {'side','gy'}, dimensions={0} | all-to-all | bytes 131072 | tf_op jit(solution)/shard_map/all_to_all | solution.py:509
  20.3 0.0 collective-permute-done.left_ref
  20.3 0.0 collective-permute-done.1.right_ref
  20.3 0.2 shard_map.60
  20.5 3.5 %collective-permute-start.4 = (f32[22,16,128]{2,1,0:T(8,128)S(1)}, f32[22,16,128]{2,1,0:T(8,128)S(1)}, u32[]{:S(2)}, u32[]{:S(2)}) collective-permute-start(f32[22,16,128]{2,1,0:T(8,128)S(1)} %get-tuple-element.12), channel_id=1, source_target_pairs={{0,4},{4,8},{8,12},{12,0},{1,5},{5,9},{9,13},{13,1},{2,6},{6,10},{... | collective-permute-start | bytes 540680 | tf_op jit(solution)/shard_map/ppermute | solution.py:517
  24.0 0.0 collective-permute-start.5
  24.0 0.0 copy-done.3
  24.0 1.2 %shard_map.62 = f32[32,32,64]{2,1,0:T(8,128)} custom-call(f32[8,16,128]{2,1,0:T(8,128)S(1)} %all_to_all.5.got_ref, f32[32,32,64]{2,1,0:T(8,128)S(1)} %copy-done.1, f32[32,64]{1,0:T(8,128)S(1)} %copy-done.3), custom_call_target="tpu_custom_call" | custom-call | tf_op jit(solution)/shard_map/pallas_call | solution.py:519
  25.2 2.4 %collective-permute-done.4.clow_ref = f32[22,16,128]{2,1,0:T(8,128)S(1)} collective-permute-done((f32[22,16,128]{2,1,0:T(8,128)S(1)}, f32[22,16,128]{2,1,0:T(8,128)S(1)}, u32[]{:S(2)}, u32[]{:S(2)}) %collective-permute-start.4) | collective-permute-done | bytes 180256 | tf_op jit(solution)/shard_map/ppermute | solution.py:517
  27.5 1.5 %collective-permute-done.5.chigh_ref = f32[22,16,128]{2,1,0:T(8,128)S(1)} collective-permute-done((f32[22,16,128]{2,1,0:T(8,128)S(1)}, f32[22,16,128]{2,1,0:T(8,128)S(1)}, u32[]{:S(2)}, u32[]{:S(2)}) %collective-permute-start.5) | collective-permute-done | bytes 180256 | tf_op jit(solution)/shard_map/ppermute | solution.py:518
  29.1 0.0 collective-permute-done.2.low_ref
  29.1 0.0 collective-permute-done.3.high_ref
  29.1 17.7 %shard_map.61 = f32[19,4,32,128]{3,2,1,0:T(8,128)} custom-call(f32[19,4,32,128]{3,2,1,0:T(8,128)S(1)} %bitcast.6, s32[4,32,128]{2,1,0:T(8,128)S(1)} %bitcast.8, f32[2,32,128]{2,1,0:T(8,128)S(1)} %get-tuple-element.11.water_ref, f32[20,4,16,128]{3,2,1,0:T(8,128)S(1)} %collective-permute-done.2.low_ref, ...), custom_call_target="tpu_custom_call" | custom-call | flops 268435456 | bytes 8388608 | tf_op jit(solution)/shard_map/pallas_call | solution.py:524
  (4 shorter events, 0.0 us)
Async XLA Ops:
  0.6 1.4 %copy-start.2 = (s32[1,4,32,128]{3,2,1,0:T(8,128)S(1)}, s32[1,4,32,128]{3,2,1,0:T(8,128)}, u32[]{:S(2)}) copy-start(s32[1,4,32,128]{3,2,1,0:T(8,128)} %param.5) | copy-start | bytes 196612
  2.1 4.4 %copy-start.1 = (f32[32,32,64]{2,1,0:T(8,128)S(1)}, f32[32,32,64]{2,1,0:T(8,128)}, u32[]{:S(2)}) copy-start(f32[32,32,64]{2,1,0:T(8,128)} %sheet_ref.1) | copy-start | bytes 786436
  2.1 4.4 %copy-start = (f32[1,19,4,32,128]{4,3,2,1,0:T(8,128)S(1)}, f32[1,19,4,32,128]{4,3,2,1,0:T(8,128)}, u32[]{:S(2)}) copy-start(f32[1,19,4,32,128]{4,3,2,1,0:T(8,128)} %param.4) | copy-start | bytes 3735556
  3.0 26.1 %collective-permute-start.2 = (f32[20,4,16,128]{3,2,1,0:T(8,128)}, f32[20,4,16,128]{3,2,1,0:T(8,128)S(1)}, u32[]{:S(2)}, u32[]{:S(2)}) collective-permute-start(f32[20,4,16,128]{3,2,1,0:T(8,128)} %pad_maximum_fusion), channel_id=1, source_target_pairs={{0,4},{4,8},{8,12},{12,0},{1,5},{5,9},{9,13},{13,1},{2,6},{6,10},{... | collective-permute-start | bytes 1966088 | tf_op jit(solution)/shard_map/ppermute | solution.py:495
  6.5 17.5 %copy-start.3 = (f32[32,64]{1,0:T(8,128)S(1)}, f32[32,64]{1,0:T(8,128)}, u32[]{:S(2)}) copy-start(f32[32,64]{1,0:T(8,128)} %current_ref.1) | copy-start | bytes 24580
  6.5 22.6 %collective-permute-start.3 = (f32[20,4,16,128]{3,2,1,0:T(8,128)}, f32[20,4,16,128]{3,2,1,0:T(8,128)S(1)}, u32[]{:S(2)}, u32[]{:S(2)}) collective-permute-start(f32[20,4,16,128]{3,2,1,0:T(8,128)} %pad_maximum_fusion.1), channel_id=1, source_target_pairs={{0,12},{4,0},{8,4},{12,8},{1,13},{5,1},{9,5},{13,9},{2,14},{6,2},{... | collective-permute-start | bytes 1966088 | tf_op jit(solution)/shard_map/ppermute | solution.py:496
  7.3 13.0 %collective-permute-start = (f32[20,16,128]{2,1,0:T(8,128)S(1)}, f32[20,16,128]{2,1,0:T(8,128)S(1)}, u32[]{:S(2)}, u32[]{:S(2)}) collective-permute-start(f32[20,16,128]{2,1,0:T(8,128)S(1)} %get-tuple-element.9), channel_id=1, source_target_pairs={{0,1},{1,2},{2,3},{3,0},{4,5},{5,6},{6,7},{7,4},{8,9},{9,10},{10,1... | collective-permute-start | bytes 491528 | tf_op jit(solution)/shard_map/ppermute | solution.py:507
  8.6 11.7 %collective-permute-start.1 = (f32[20,16,128]{2,1,0:T(8,128)S(1)}, f32[20,16,128]{2,1,0:T(8,128)S(1)}, u32[]{:S(2)}, u32[]{:S(2)}) collective-permute-start(f32[20,16,128]{2,1,0:T(8,128)S(1)} %get-tuple-element.10), channel_id=1, source_target_pairs={{0,3},{1,0},{2,1},{3,2},{4,7},{5,4},{6,5},{7,6},{8,11},{9,8},{10,9... | collective-permute-start | bytes 491528 | tf_op jit(solution)/shard_map/ppermute | solution.py:508
  20.5 7.0 %collective-permute-start.4 = (f32[22,16,128]{2,1,0:T(8,128)S(1)}, f32[22,16,128]{2,1,0:T(8,128)S(1)}, u32[]{:S(2)}, u32[]{:S(2)}) collective-permute-start(f32[22,16,128]{2,1,0:T(8,128)S(1)} %get-tuple-element.12), channel_id=1, source_target_pairs={{0,4},{4,8},{8,12},{12,0},{1,5},{5,9},{9,13},{13,1},{2,6},{6,10},{... | collective-permute-start | bytes 540680 | tf_op jit(solution)/shard_map/ppermute | solution.py:517
  24.0 5.1 %collective-permute-start.5 = (f32[22,16,128]{2,1,0:T(8,128)S(1)}, f32[22,16,128]{2,1,0:T(8,128)S(1)}, u32[]{:S(2)}, u32[]{:S(2)}) collective-permute-start(f32[22,16,128]{2,1,0:T(8,128)S(1)} %get-tuple-element.13), channel_id=1, source_target_pairs={{0,12},{4,0},{8,4},{12,8},{1,13},{5,1},{9,5},{13,9},{2,14},{6,2},{... | collective-permute-start | bytes 540680 | tf_op jit(solution)/shard_map/ppermute | solution.py:518

commit v4 on v3

--- a/solution.py
+++ b/solution.py
@@ -198,10 +198,12 @@
         if step:
             last = 2 * (step - 1) + TILE * (tiles_of(step - 1) - 1)
             for window in range(WINDOWS):
+                gather(last, window, half)
+            for window in range(WINDOWS):
                 collide(first, window, half)
             for window in range(WINDOWS):
                 fold(last - TILE, window, half)
-                gather(last, window, half)
+            for window in range(WINDOWS):
                 fold(last, window, half)
         else:
             for window in range(WINDOWS):
@@ -353,11 +355,37 @@
     finish(out_ref, refs, layers, height)
 
 
-def strip_kernel(me_ref, f_ref, mask_ref, ends_ref, left_ref, right_ref, payload_ref):
+def pack_kernel(me_ref, f_hbm, mask_hbm, sheet_hbm, last_ref, first_ref, left_ref, right_ref, payload_ref,
+                f_ref, mask_ref, cells_ref, ends_ref, sems):
     layers, height = f_ref.shape[1], f_ref.shape[2]
     lane = lane_index()
     half_rows = height // 2
     half_lanes = LANES // 2
+    columns = cells_ref.shape[2]
+
+    load = pltpu.make_async_copy(f_hbm, f_ref, sems.at[0])
+    load.start()
+    load_mask = pltpu.make_async_copy(mask_hbm, mask_ref, sems.at[1])
+    load_mask.start()
+    loads = [
+        pltpu.make_async_copy(sheet_hbm.at[cell], cells_ref.at[which], sems.at[2 + which])
+        for which, cell in enumerate((0, sheet_hbm.shape[0] - 1))
+    ]
+    for copy in loads:
+        copy.start()
+    for copy in loads:
+        copy.wait()
+    ends_ref[...] = jnp.zeros(ends_ref.shape, jnp.float32)
+    for which in range(2):
+        ends_ref[which, :, :columns] = cells_ref[which]
+    load_mask.wait()
+    load.wait()
+
+    for i in range(DIRS):
+        last_ref[i] = f_ref[i, :, height - HALO :, :]
+        first_ref[i] = f_ref[i, :, :HALO, :]
+    last_ref[DIRS] = mask_ref[:, height - HALO :, :].astype(jnp.float32)
+    first_ref[DIRS] = mask_ref[:, :HALO, :].astype(jnp.float32)
 
     def pack(i, read):
         for t in range(half_rows // TILE):
@@ -484,26 +512,28 @@
     layers, height, width = lattice.shape[1:]
     groups = lax.axis_size(("side", "gy"))
     f32 = jnp.float32
-    mask_values = solids.astype(f32)[None]
 
     def shape(*dims):
         return jax.ShapeDtypeStruct(dims, f32)
 
-    def rows_of(cut):
-        return jnp.concatenate([lattice[:, :, cut], mask_values[:, :, cut]])
-
-    low = lax.ppermute(rows_of(slice(height - HALO, height)), "gx", ring("gx", 1))
-    high = lax.ppermute(rows_of(slice(0, HALO)), "gx", ring("gx", -1))
-
-    ends = jnp.stack([water_sheet[0], water_sheet[-1]])
-    ends = jnp.pad(ends, ((0, 0), (0, 0), (0, LANES - ends.shape[2])))
     me = lax.axis_index(("side", "gy")).reshape(1)
     strip = shape(DIRS + 1, height // 2, LANES)
-    send_left, send_right, payload = pl.pallas_call(
-        strip_kernel, out_shape=(strip, strip, shape(groups, 2 * TILE, LANES)),
-        in_specs=[pl.BlockSpec(memory_space=pltpu.SMEM), VMEM, VMEM, VMEM], out_specs=(VMEM,) * 3,
-        compiler_params=pltpu.CompilerParams(vmem_limit_bytes=8 << 20),
-    )(me, lattice, solids, ends)
+    band = shape(DIRS + 1, layers, HALO, width)
+    send_last, send_first, send_left, send_right, payload = pl.pallas_call(
+        pack_kernel, out_shape=(band, band, strip, strip, shape(groups, 2 * TILE, LANES)),
+        in_specs=[pl.BlockSpec(memory_space=pltpu.SMEM)] + [pl.BlockSpec(memory_space=pltpu.HBM)] * 3,
+        out_specs=(VMEM,) * 5,
+        scratch_shapes=[
+            pltpu.VMEM(lattice.shape, f32),
+            pltpu.VMEM(solids.shape, jnp.int32),
+            pltpu.VMEM((2,) + water_sheet.shape[1:], f32),
+            pltpu.VMEM((2, height, width), f32),
+            pltpu.SemaphoreType.DMA((4,)),
+        ],
+        compiler_params=pltpu.CompilerParams(vmem_limit_bytes=62000000),
+    )(me, lattice, solids, water_sheet)
+    low = lax.ppermute(send_last, "gx", ring("gx", 1))
+    high = lax.ppermute(send_first, "gx", ring("gx", -1))
     left = lax.ppermute(send_right, "gy", ring("gy", 1))
     right = lax.ppermute(send_left, "gy", ring("gy", -1))
     got = lax.all_to_all(payload, ("side", "gy"), split_axis=0, concat_axis=0, tiled=True)

time: 47 us -> 46.5 us (0.989)
  Pallas kernels: 19.9 us -> 22.2 us
  other arithmetic: 1.8 us -> 0 us
  local copies, waits for them, and re-layouts: 1.43 us -> 0.02 us
    pallas_call x1, Pallas kernels: 0.75 us -> 3.21 us  [on_device(): pl.pallas_call(pack_kernel, out_shape=(band, band, strip, strip, shape(gr...]
    concatenate x2 -> x0, other arithmetic: 1.79 us -> none  [rows_of(): return jnp.concatenate([lattice[:, :, cut], mask_values[:, :, cut]])]
    slice x3 -> x0, local copies, waits for them, and re-layouts: 1.41 us -> none  [the longest x2 1.41 us: rows_of(): return jnp.concatenate([lattice[:, :, cut], mask_values[:, :, cut]])]
  transfers between devices with their start and end apart: 6 -> 6, of which waited for: 2 -> 2; matrix products, arithmetic and copies ran while one was open for 2% -> 0% of each run, Pallas kernels for 5% -> 3%
where the time goes in v4:
time: 46.5 us; the launch traced here: 46.1 us
  Pallas kernels  22.2 us (48%)
  blocking collectives  9.84 us (21%)
  starting transfers between devices  9.45 us (20%)
  waiting for transfers between devices  3.89 us (8%)
  between operations  0.71 us (2%)
    pallas_call x1, Pallas kernels, on_device(): pl.pallas_call(lattice_kernel, out_shape=shape(*lattice.shape), in_specs=...  17.7 us
    all_to_all x1, blocking collectives, on_device(): lax.all_to_all(payload, ('side', 'gy'), split_axis=0, concat_axis=0, tile...  9.84 us
    ppermute x1, starting transfers between devices, on_device(): corner_low = lax.ppermute(send_up, 'gx', ring('gx', 1))  3.48 us
    pallas_call x1, Pallas kernels, on_device(): pl.pallas_call(pack_kernel, out_shape=(band, band, strip, strip, shape(gr...  3.21 us
    ppermute x1, starting transfers between devices, on_device(): low = lax.ppermute(send_last, 'gx', ring('gx', 1))  2.64 us
    ppermute x1, waiting for transfers between devices, on_device(): corner_low = lax.ppermute(send_up, 'gx', ring('gx', 1))  2.35 us
    ppermute x1, starting transfers between devices, on_device(): right = lax.ppermute(send_left, 'gy', ring('gy', -1))  2.03 us
    ppermute x1, waiting for transfers between devices, on_device(): corner_high = lax.ppermute(send_down, 'gx', ring('gx', -1))  1.53 us
  transfers between devices with their start and end apart: 6, of which 2 were waited for; matrix products, arithmetic and copies ran while one was open for 0% of the time, Pallas kernels for 3%

profile of v4, /device:TPU:1, one launch (start us, length us, event | category | flops | bytes accessed | tf_op | source)
XLA Modules:
  0.0 46.1 jit_solution(16556050634119906489)
XLA Ops:
  0.6 0.0 copy-start.1
  0.6 0.0 copy-start.3
  0.7 3.2 %shard_map.59 = (f32[20,4,16,128]{3,2,1,0:T(8,128)}, f32[20,4,16,128]{3,2,1,0:T(8,128)}, f32[20,16,128]{2,1,0:T(8,128)}, f32[20,16,128]{2,1,0:T(8,128)}, f32[8,16,128]{2,1,0:T(8,128)}) custom-call(s32[1]{0:T(128)} %bitcast.2.me_ref, f32[19,4,32,128]{3,2,1,0:T(8,128)} %bitcast.4, s32[4,32,128]{2,1,0:T(8,128)} %bitcast.6, f32[32,32,64]{2,1,0:T(8,128)} %sheet_ref.1), custom_call_target="tpu_custom_call" | custom-call | tf_op jit(solution)/shard_map/pallas_call | solution.py:522
  3.9 0.0 copy-start
  3.9 0.0 copy-start.2
  3.9 2.6 %collective-permute-start.2 = (f32[20,4,16,128]{3,2,1,0:T(8,128)}, f32[20,4,16,128]{3,2,1,0:T(8,128)S(1)}, u32[]{:S(2)}, u32[]{:S(2)}) collective-permute-start(f32[20,4,16,128]{3,2,1,0:T(8,128)} %get-tuple-element.14), channel_id=1, source_target_pairs={{0,4},{4,8},{8,12},{12,0},{1,5},{5,9},{9,13},{13,1},{2,6},{6,10},{... | collective-permute-start | bytes 1966088 | tf_op jit(solution)/shard_map/ppermute | solution.py:535
  6.5 0.0 collective-permute-start.3
  6.5 1.3 %collective-permute-start = (f32[20,16,128]{2,1,0:T(8,128)}, f32[20,16,128]{2,1,0:T(8,128)S(1)}, u32[]{:S(2)}, u32[]{:S(2)}) collective-permute-start(f32[20,16,128]{2,1,0:T(8,128)} %get-tuple-element.11), channel_id=1, source_target_pairs={{0,1},{1,2},{2,3},{3,0},{4,5},{5,6},{6,7},{7,4},{8,9},{9,10},{10,1... | collective-permute-start | bytes 491528 | tf_op jit(solution)/shard_map/ppermute | solution.py:537
  7.8 2.0 %collective-permute-start.1 = (f32[20,16,128]{2,1,0:T(8,128)}, f32[20,16,128]{2,1,0:T(8,128)S(1)}, u32[]{:S(2)}, u32[]{:S(2)}) collective-permute-start(f32[20,16,128]{2,1,0:T(8,128)} %get-tuple-element.12), channel_id=1, source_target_pairs={{0,3},{1,0},{2,1},{3,2},{4,7},{5,4},{6,5},{7,6},{8,11},{9,8},{10,9... | collective-permute-start | bytes 491528 | tf_op jit(solution)/shard_map/ppermute | solution.py:538
  9.9 9.8 %all_to_all.5.got_ref = f32[8,16,128]{2,1,0:T(8,128)S(1)} all-to-all(f32[8,16,128]{2,1,0:T(8,128)} %get-tuple-element.10), channel_id=1, replica_groups=mesh['side'=2,'gx'=4,'gy'=4] {'side','gy'}, dimensions={0} | all-to-all | bytes 131072 | tf_op jit(solution)/shard_map/all_to_all | solution.py:539
  19.7 0.0 collective-permute-done.left_ref
  19.7 0.0 collective-permute-done.1.right_ref
  19.7 0.2 shard_map.60
  19.9 3.5 %collective-permute-start.4 = (f32[22,16,128]{2,1,0:T(8,128)S(1)}, f32[22,16,128]{2,1,0:T(8,128)S(1)}, u32[]{:S(2)}, u32[]{:S(2)}) collective-permute-start(f32[22,16,128]{2,1,0:T(8,128)S(1)} %get-tuple-element.16), channel_id=1, source_target_pairs={{0,4},{4,8},{8,12},{12,0},{1,5},{5,9},{9,13},{13,1},{2,6},{6,10},{... | collective-permute-start | bytes 540680 | tf_op jit(solution)/shard_map/ppermute | solution.py:547
  23.4 0.0 collective-permute-start.5
  23.4 0.0 copy-done.1
  23.4 0.0 copy-done.3
  23.4 1.2 %shard_map.62 = f32[32,32,64]{2,1,0:T(8,128)} custom-call(f32[8,16,128]{2,1,0:T(8,128)S(1)} %all_to_all.5.got_ref, f32[32,32,64]{2,1,0:T(8,128)S(1)} %copy-done.1, f32[32,64]{1,0:T(8,128)S(1)} %copy-done.3), custom_call_target="tpu_custom_call" | custom-call | tf_op jit(solution)/shard_map/pallas_call | solution.py:549
  24.6 2.3 %collective-permute-done.4.clow_ref = f32[22,16,128]{2,1,0:T(8,128)S(1)} collective-permute-done((f32[22,16,128]{2,1,0:T(8,128)S(1)}, f32[22,16,128]{2,1,0:T(8,128)S(1)}, u32[]{:S(2)}, u32[]{:S(2)}) %collective-permute-start.4) | collective-permute-done | bytes 180256 | tf_op jit(solution)/shard_map/ppermute | solution.py:547
  26.9 1.5 %collective-permute-done.5.chigh_ref = f32[22,16,128]{2,1,0:T(8,128)S(1)} collective-permute-done((f32[22,16,128]{2,1,0:T(8,128)S(1)}, f32[22,16,128]{2,1,0:T(8,128)S(1)}, u32[]{:S(2)}, u32[]{:S(2)}) %collective-permute-start.5) | collective-permute-done | bytes 180256 | tf_op jit(solution)/shard_map/ppermute | solution.py:548
  28.5 0.0 collective-permute-done.2.low_ref
  28.5 0.0 collective-permute-done.3.high_ref
  28.5 0.0 copy-done
  28.5 0.0 copy-done.2
  28.5 17.7 %shard_map.61 = f32[19,4,32,128]{3,2,1,0:T(8,128)} custom-call(f32[19,4,32,128]{3,2,1,0:T(8,128)S(1)} %bitcast.5, s32[4,32,128]{2,1,0:T(8,128)S(1)} %bitcast.7, f32[2,32,128]{2,1,0:T(8,128)S(1)} %get-tuple-element.13.water_ref, f32[20,4,16,128]{3,2,1,0:T(8,128)S(1)} %collective-permute-done.2.low_ref, ...), custom_call_target="tpu_custom_call" | custom-call | flops 268435456 | bytes 8388608 | tf_op jit(solution)/shard_map/pallas_call | solution.py:554
Async XLA Ops:
  0.6 22.8 %copy-start.1 = (f32[32,32,64]{2,1,0:T(8,128)S(1)}, f32[32,32,64]{2,1,0:T(8,128)}, u32[]{:S(2)}) copy-start(f32[32,32,64]{2,1,0:T(8,128)} %sheet_ref.1) | copy-start | bytes 786436
  0.6 22.8 %copy-start.3 = (f32[32,64]{1,0:T(8,128)S(1)}, f32[32,64]{1,0:T(8,128)}, u32[]{:S(2)}) copy-start(f32[32,64]{1,0:T(8,128)} %current_ref.1) | copy-start | bytes 24580
  3.9 24.6 %copy-start = (f32[1,19,4,32,128]{4,3,2,1,0:T(8,128)S(1)}, f32[1,19,4,32,128]{4,3,2,1,0:T(8,128)}, u32[]{:S(2)}) copy-start(f32[1,19,4,32,128]{4,3,2,1,0:T(8,128)} %param.4) | copy-start | bytes 3735556
  3.9 24.6 %copy-start.2 = (s32[1,4,32,128]{3,2,1,0:T(8,128)S(1)}, s32[1,4,32,128]{3,2,1,0:T(8,128)}, u32[]{:S(2)}) copy-start(s32[1,4,32,128]{3,2,1,0:T(8,128)} %param.5) | copy-start | bytes 196612
  3.9 24.6 %collective-permute-start.2 = (f32[20,4,16,128]{3,2,1,0:T(8,128)}, f32[20,4,16,128]{3,2,1,0:T(8,128)S(1)}, u32[]{:S(2)}, u32[]{:S(2)}) collective-permute-start(f32[20,4,16,128]{3,2,1,0:T(8,128)} %get-tuple-element.14), channel_id=1, source_target_pairs={{0,4},{4,8},{8,12},{12,0},{1,5},{5,9},{9,13},{13,1},{2,6},{6,10},{... | collective-permute-start | bytes 1966088 | tf_op jit(solution)/shard_map/ppermute | solution.py:535
  6.5 21.9 %collective-permute-start.3 = (f32[20,4,16,128]{3,2,1,0:T(8,128)}, f32[20,4,16,128]{3,2,1,0:T(8,128)S(1)}, u32[]{:S(2)}, u32[]{:S(2)}) collective-permute-start(f32[20,4,16,128]{3,2,1,0:T(8,128)} %get-tuple-element.15), channel_id=1, source_target_pairs={{0,12},{4,0},{8,4},{12,8},{1,13},{5,1},{9,5},{13,9},{2,14},{6,2},{... | collective-permute-start | bytes 1966088 | tf_op jit(solution)/shard_map/ppermute | solution.py:536
  6.5 13.2 %collective-permute-start = (f32[20,16,128]{2,1,0:T(8,128)}, f32[20,16,128]{2,1,0:T(8,128)S(1)}, u32[]{:S(2)}, u32[]{:S(2)}) collective-permute-start(f32[20,16,128]{2,1,0:T(8,128)} %get-tuple-element.11), channel_id=1, source_target_pairs={{0,1},{1,2},{2,3},{3,0},{4,5},{5,6},{6,7},{7,4},{8,9},{9,10},{10,1... | collective-permute-start | bytes 491528 | tf_op jit(solution)/shard_map/ppermute | solution.py:537
  7.8 11.9 %collective-permute-start.1 = (f32[20,16,128]{2,1,0:T(8,128)}, f32[20,16,128]{2,1,0:T(8,128)S(1)}, u32[]{:S(2)}, u32[]{:S(2)}) collective-permute-start(f32[20,16,128]{2,1,0:T(8,128)} %get-tuple-element.12), channel_id=1, source_target_pairs={{0,3},{1,0},{2,1},{3,2},{4,7},{5,4},{6,5},{7,6},{8,11},{9,8},{10,9... | collective-permute-start | bytes 491528 | tf_op jit(solution)/shard_map/ppermute | solution.py:538
  19.9 7.0 %collective-permute-start.4 = (f32[22,16,128]{2,1,0:T(8,128)S(1)}, f32[22,16,128]{2,1,0:T(8,128)S(1)}, u32[]{:S(2)}, u32[]{:S(2)}) collective-permute-start(f32[22,16,128]{2,1,0:T(8,128)S(1)} %get-tuple-element.16), channel_id=1, source_target_pairs={{0,4},{4,8},{8,12},{12,0},{1,5},{5,9},{9,13},{13,1},{2,6},{6,10},{... | collective-permute-start | bytes 540680 | tf_op jit(solution)/shard_map/ppermute | solution.py:547
  23.4 5.1 %collective-permute-start.5 = (f32[22,16,128]{2,1,0:T(8,128)S(1)}, f32[22,16,128]{2,1,0:T(8,128)S(1)}, u32[]{:S(2)}, u32[]{:S(2)}) collective-permute-start(f32[22,16,128]{2,1,0:T(8,128)S(1)} %get-tuple-element.17), channel_id=1, source_target_pairs={{0,12},{4,0},{8,4},{12,8},{1,13},{5,1},{9,5},{13,9},{2,14},{6,2},{... | collective-permute-start | bytes 540680 | tf_op jit(solution)/shard_map/ppermute | solution.py:548

commit v5 on v4

--- a/solution.py
+++ b/solution.py
@@ -277,7 +277,7 @@
                 out_ref[2 * k + 2, z, to, :] = even - odd
         return carry
 
-    lax.fori_loop(0, height // TILE, tile_out, 0)
+    lax.fori_loop(0, height // TILE, tile_out, 0, unroll=2)
 
 
 def window_scratch(layers, rows):
@@ -296,7 +296,39 @@
     return [(part[0], (part[1:7], part[7:13])) + tuple(part[13:]) for part in parts]
 
 
-def lattice_kernel(f_ref, mask_ref, water_ref, low_ref, high_ref, left_ref, right_ref, clow_ref,
+def edges_kernel(f_ref, mask_ref, low_ref, high_ref, left_ref, right_ref, out_ref):
+    layers, height = f_ref.shape[1], f_ref.shape[2]
+    lane = lane_index()
+    move = 3 * HALO
+    left_at = 2 * HALO
+    half_tiles = height // TILE // 2
+    at_end = lane >= LANES - 2 * HALO
+    at_left = (lane >= left_at) & (lane < left_at + HALO)
+    at_right = lane < HALO
+
+    def own(tile):
+        return jnp.where(at_end, tile, spin(tile, move))
+
+    for i in range(DIRS + 1):
+        for z in range(layers):
+            for t in range(HALO // TILE):
+                rows = slice(TILE * t, TILE * (t + 1))
+                out_ref[i, z, rows, :] = own(low_ref[i, z, rows, :])
+                after = slice(HALO + height + TILE * t, HALO + height + TILE * (t + 1))
+                out_ref[i, z, after, :] = own(high_ref[i, z, rows, :])
+            for t in range(height // TILE):
+                own_rows = slice(TILE * t, TILE * (t + 1))
+                rows = slice(TILE * (t % half_tiles), TILE * (t % half_tiles) + TILE)
+                at = LANES // 2 * (t // half_tiles) + HALO * z
+                tile = f_ref[i, z, own_rows, :] if i < DIRS else mask_ref[z, own_rows, :].astype(jnp.float32)
+                right = spin(right_ref[i, rows, :], -at)
+                left = spin(left_ref[i, rows, :], left_at - at)
+                out_ref[i, z, HALO + TILE * t : HALO + TILE * (t + 1), :] = jnp.where(
+                    at_right, right, jnp.where(at_left, left, own(tile))
+                )
+
+
+def lattice_kernel(f_ref, mask_ref, water_ref, low_ref, high_ref, edges_ref, clow_ref,
                    chigh_ref, out_ref, *scratch):
     refs = window_refs(scratch)
     layers, height = f_ref.shape[1], f_ref.shape[2]
@@ -305,28 +337,22 @@
     left_at = 2 * HALO
     low_tiles = HALO // TILE
     mid_tiles = height // TILE
-    half_tiles = mid_tiles // 2
     half_lanes = LANES // 2
     at_end = lane >= LANES - 2 * HALO
     at_left = (lane >= left_at) & (lane < left_at + HALO)
     at_right = lane < HALO
 
-    def join(own, left, right):
-        return jnp.where(at_end, own, jnp.where(at_right, right, jnp.where(at_left, left, spin(own, move))))
-
     for tile in range(2 * low_tiles + mid_tiles):
+        window_rows = slice(TILE * tile, TILE * (tile + 1))
         if low_tiles <= tile < low_tiles + mid_tiles:
             t = tile - low_tiles
             own_rows = slice(TILE * t, TILE * (t + 1))
-            rows = slice(TILE * (t % half_tiles), TILE * (t % half_tiles) + TILE)
-            first = half_lanes * (t // half_tiles)
 
             def own_of(i, z, own_rows=own_rows):
                 return f_ref[i, z, own_rows, :] if i < DIRS else mask_ref[z, own_rows, :].astype(jnp.float32)
 
-            def halo(i, z, rows=rows, first=first):
-                at = first + HALO * z
-                return spin(left_ref[i, rows, :], left_at - at), spin(right_ref[i, rows, :], -at)
+            def edge_of(i, z, window_rows=window_rows):
+                return edges_ref[i, z, window_rows, :]
 
             own, extra = (water_ref[k, own_rows, :] for k in range(2))
         else:
@@ -337,17 +363,18 @@
             def own_of(i, z, rows=rows, own_ref=own_ref):
                 return own_ref[i, z, rows, :]
 
-            def halo(i, z, rows=rows, corner_ref=corner_ref):
+            def edge_of(i, z, rows=rows, corner_ref=corner_ref, window_rows=window_rows):
                 both = corner_ref[i, rows, :]
-                return spin(both, left_at - HALO * z), spin(both, -half_lanes - HALO * z)
+                left, right = spin(both, left_at - HALO * z), spin(both, -half_lanes - HALO * z)
+                return jnp.where(at_right, right, jnp.where(at_left, left, edges_ref[i, z, window_rows, :]))
 
             own, extra = (corner_ref[DIRS + 1 + k, rows, :] for k in range(2))
 
-        def edge_of(i, z, own_of=own_of, halo=halo):
-            return join(own_of(i, z), *halo(i, z))
-
-        refs[0][5][FRONT + TILE * tile : FRONT + TILE * (tile + 1), :] = own
-        refs[1][5][FRONT + TILE * tile : FRONT + TILE * (tile + 1), :] = join(own, spin(extra, move), extra)
+        framed = slice(FRONT + TILE * tile, FRONT + TILE * (tile + 1))
+        refs[0][5][framed, :] = own
+        refs[1][5][framed, :] = jnp.where(
+            at_end, own, jnp.where(at_right, extra, jnp.where(at_left, spin(extra, move), spin(own, move)))
+        )
         begin(own_of, lambda z, f=own_of: f(DIRS, z), TILE * tile, 0, layers, refs)
         begin(edge_of, lambda z, f=edge_of: f(DIRS, z), TILE * tile, 1, layers, refs)
     first_folds(refs, layers, height + 2 * HALO)
@@ -551,13 +578,18 @@
         in_specs=[VMEM] * 3, out_specs=VMEM,
         compiler_params=pltpu.CompilerParams(vmem_limit_bytes=8 << 20),
     )(got, water_sheet, current)
+    edges = pl.pallas_call(
+        edges_kernel, out_shape=shape(DIRS + 1, layers, height + 2 * HALO, LANES),
+        in_specs=[VMEM] * 6, out_specs=VMEM,
+        compiler_params=pltpu.CompilerParams(vmem_limit_bytes=8 << 20),
+    )(lattice, solids, low, high, left, right)
     out = pl.pallas_call(
         lattice_kernel, out_shape=shape(*lattice.shape),
-        in_specs=[VMEM] * 9, out_specs=VMEM,
+        in_specs=[VMEM] * 8, out_specs=VMEM,
         compiler_params=pltpu.CompilerParams(vmem_limit_bytes=36 << 20),
         scratch_shapes=window_scratch(layers, height + 2 * HALO),
         cost_estimate=pl.CostEstimate(flops=1 << 28, bytes_accessed=8 << 20, transcendentals=0),
-    )(lattice, solids, water_here, low, high, left, right, corner_low, corner_high)
+    )(lattice, solids, water_here, low, high, edges, corner_low, corner_high)
     return (out[None], water)
 
 

time: 46.5 us -> 45.2 us (0.972)
  waiting for transfers between devices: 3.89 us -> 2.53 us
    ppermute x1, waiting for transfers between devices: 2.35 us -> 0.99 us  [on_device(): corner_low = lax.ppermute(send_up, 'gx', ring('gx', 1))]
    pallas_call x0 -> x1, Pallas kernels: none -> 1.33 us  [on_device(): pl.pallas_call(edges_kernel, out_shape=shape(DIRS + 1, layers, height + 2...]
    pallas_call x1, Pallas kernels: 17.7 us -> 16.4 us  [on_device(): pl.pallas_call(lattice_kernel, out_shape=shape(*lattice.shape), in_specs=...]
  transfers between devices with their start and end apart: 6 -> 6, of which waited for: 2 -> 2; matrix products, arithmetic and copies ran while one was open for 0% -> 0% of each run, Pallas kernels for 3% -> 6%
where the time goes in v5:
time: 45.2 us; the launch traced here: 44.9 us
  Pallas kernels  22.3 us (49%)
  blocking collectives  9.84 us (22%)
  starting transfers between devices  9.45 us (21%)
  waiting for transfers between devices  2.53 us (6%)
  between operations  0.71 us (2%)
    pallas_call x1, Pallas kernels, on_device(): pl.pallas_call(lattice_kernel, out_shape=shape(*lattice.shape), in_specs=...  16.4 us
    all_to_all x1, blocking collectives, on_device(): lax.all_to_all(payload, ('side', 'gy'), split_axis=0, concat_axis=0, tile...  9.84 us
    ppermute x1, starting transfers between devices, on_device(): corner_low = lax.ppermute(send_up, 'gx', ring('gx', 1))  3.48 us
    pallas_call x1, Pallas kernels, on_device(): pl.pallas_call(pack_kernel, out_shape=(band, band, strip, strip, shape(gr...  3.21 us
    ppermute x1, starting transfers between devices, on_device(): low = lax.ppermute(send_last, 'gx', ring('gx', 1))  2.64 us
    ppermute x1, starting transfers between devices, on_device(): right = lax.ppermute(send_left, 'gy', ring('gy', -1))  2.03 us
    ppermute x1, waiting for transfers between devices, on_device(): corner_high = lax.ppermute(send_down, 'gx', ring('gx', -1))  1.53 us
    pallas_call x1, Pallas kernels, on_device(): pl.pallas_call(edges_kernel, out_shape=shape(DIRS + 1, layers, height + 2...  1.33 us
  transfers between devices with their start and end apart: 6, of which 2 were waited for; matrix products, arithmetic and copies ran while one was open for 0% of the time, Pallas kernels for 6%

profile of v5, /device:TPU:1, one launch (start us, length us, event | category | flops | bytes accessed | tf_op | source)
XLA Modules:
  0.0 44.9 jit_solution(16209776348086618083)
XLA Ops:
  0.6 0.0 copy-start.1
  0.6 0.0 copy-start.3
  0.7 3.2 %shard_map.59 = (f32[20,4,16,128]{3,2,1,0:T(8,128)}, f32[20,4,16,128]{3,2,1,0:T(8,128)}, f32[20,16,128]{2,1,0:T(8,128)}, f32[20,16,128]{2,1,0:T(8,128)}, f32[8,16,128]{2,1,0:T(8,128)}) custom-call(s32[1]{0:T(128)} %bitcast.2.me_ref, f32[19,4,32,128]{3,2,1,0:T(8,128)} %bitcast.4, s32[4,32,128]{2,1,0:T(8,128)} %bitcast.7, f32[32,32,64]{2,1,0:T(8,128)} %sheet_ref.1), custom_call_target="tpu_custom_call" | custom-call | tf_op jit(solution)/shard_map/pallas_call | solution.py:549
  3.9 0.0 copy-start
  3.9 0.0 copy-start.2
  3.9 2.6 %collective-permute-start.2 = (f32[20,4,16,128]{3,2,1,0:T(8,128)}, f32[20,4,16,128]{3,2,1,0:T(8,128)S(1)}, u32[]{:S(2)}, u32[]{:S(2)}) collective-permute-start(f32[20,4,16,128]{3,2,1,0:T(8,128)} %get-tuple-element.14), channel_id=1, source_target_pairs={{0,4},{4,8},{8,12},{12,0},{1,5},{5,9},{9,13},{13,1},{2,6},{6,10},{... | collective-permute-start | bytes 1966088 | tf_op jit(solution)/shard_map/ppermute | solution.py:562
  6.5 0.0 collective-permute-start.3
  6.5 1.3 %collective-permute-start = (f32[20,16,128]{2,1,0:T(8,128)}, f32[20,16,128]{2,1,0:T(8,128)S(1)}, u32[]{:S(2)}, u32[]{:S(2)}) collective-permute-start(f32[20,16,128]{2,1,0:T(8,128)} %get-tuple-element.11), channel_id=1, source_target_pairs={{0,1},{1,2},{2,3},{3,0},{4,5},{5,6},{6,7},{7,4},{8,9},{9,10},{10,1... | collective-permute-start | bytes 491528 | tf_op jit(solution)/shard_map/ppermute | solution.py:564
  7.8 2.0 %collective-permute-start.1 = (f32[20,16,128]{2,1,0:T(8,128)}, f32[20,16,128]{2,1,0:T(8,128)S(1)}, u32[]{:S(2)}, u32[]{:S(2)}) collective-permute-start(f32[20,16,128]{2,1,0:T(8,128)} %get-tuple-element.12), channel_id=1, source_target_pairs={{0,3},{1,0},{2,1},{3,2},{4,7},{5,4},{6,5},{7,6},{8,11},{9,8},{10,9... | collective-permute-start | bytes 491528 | tf_op jit(solution)/shard_map/ppermute | solution.py:565
  9.9 9.8 %all_to_all.5.got_ref = f32[8,16,128]{2,1,0:T(8,128)S(1)} all-to-all(f32[8,16,128]{2,1,0:T(8,128)} %get-tuple-element.10), channel_id=1, replica_groups=mesh['side'=2,'gx'=4,'gy'=4] {'side','gy'}, dimensions={0} | all-to-all | bytes 131072 | tf_op jit(solution)/shard_map/all_to_all | solution.py:566
  19.7 0.0 collective-permute-done.left_ref
  19.7 0.0 collective-permute-done.1.right_ref
  19.7 0.2 shard_map.60
  19.9 3.5 %collective-permute-start.4 = (f32[22,16,128]{2,1,0:T(8,128)S(1)}, f32[22,16,128]{2,1,0:T(8,128)S(1)}, u32[]{:S(2)}, u32[]{:S(2)}) collective-permute-start(f32[22,16,128]{2,1,0:T(8,128)S(1)} %get-tuple-element.16), channel_id=1, source_target_pairs={{0,4},{4,8},{8,12},{12,0},{1,5},{5,9},{9,13},{13,1},{2,6},{6,10},{... | collective-permute-start | bytes 540680 | tf_op jit(solution)/shard_map/ppermute | solution.py:574
  23.4 0.0 collective-permute-start.5
  23.4 0.0 copy-done.1
  23.4 0.0 copy-done.3
  23.4 1.2 %shard_map.63 = f32[32,32,64]{2,1,0:T(8,128)} custom-call(f32[8,16,128]{2,1,0:T(8,128)S(1)} %all_to_all.5.got_ref, f32[32,32,64]{2,1,0:T(8,128)S(1)} %copy-done.1, f32[32,64]{1,0:T(8,128)S(1)} %copy-done.3), custom_call_target="tpu_custom_call" | custom-call | tf_op jit(solution)/shard_map/pallas_call | solution.py:576
  24.6 0.0 collective-permute-done.2.low_ref
  24.6 0.0 collective-permute-done.3.high_ref
  24.6 0.0 copy-done
  24.6 0.0 copy-done.2
  24.6 1.3 %shard_map.61.edges_ref = f32[20,4,64,128]{3,2,1,0:T(8,128)S(1)} custom-call(f32[19,4,32,128]{3,2,1,0:T(8,128)S(1)} %bitcast.5, s32[4,32,128]{2,1,0:T(8,128)S(1)} %bitcast.8, f32[20,4,16,128]{3,2,1,0:T(8,128)S(1)} %collective-permute-done.2.low_ref, f32[20,4,16,128]{3,2,1,0:T(8,128)S(1)} %collective-permute-done.3.high_ref, ...), custom_call_target="tpu_custom_call" | custom-call | tf_op jit(solution)/shard_map/pallas_call | solution.py:581
  25.9 1.0 %collective-permute-done.4.clow_ref = f32[22,16,128]{2,1,0:T(8,128)S(1)} collective-permute-done((f32[22,16,128]{2,1,0:T(8,128)S(1)}, f32[22,16,128]{2,1,0:T(8,128)S(1)}, u32[]{:S(2)}, u32[]{:S(2)}) %collective-permute-start.4) | collective-permute-done | bytes 180256 | tf_op jit(solution)/shard_map/ppermute | solution.py:574
  26.9 1.5 %collective-permute-done.5.chigh_ref = f32[22,16,128]{2,1,0:T(8,128)S(1)} collective-permute-done((f32[22,16,128]{2,1,0:T(8,128)S(1)}, f32[22,16,128]{2,1,0:T(8,128)S(1)}, u32[]{:S(2)}, u32[]{:S(2)}) %collective-permute-start.5) | collective-permute-done | bytes 180256 | tf_op jit(solution)/shard_map/ppermute | solution.py:575
  28.5 16.4 %shard_map.62 = f32[19,4,32,128]{3,2,1,0:T(8,128)} custom-call(f32[19,4,32,128]{3,2,1,0:T(8,128)S(1)} %bitcast.6, s32[4,32,128]{2,1,0:T(8,128)S(1)} %bitcast.9, f32[2,32,128]{2,1,0:T(8,128)S(1)} %get-tuple-element.13.water_ref, f32[20,4,16,128]{3,2,1,0:T(8,128)S(1)} %collective-permute-done.2.low_ref, ...), custom_call_target="tpu_custom_call" | custom-call | flops 268435456 | bytes 8388608 | tf_op jit(solution)/shard_map/pallas_call | solution.py:586
Async XLA Ops:
  0.6 22.8 %copy-start.1 = (f32[32,32,64]{2,1,0:T(8,128)S(1)}, f32[32,32,64]{2,1,0:T(8,128)}, u32[]{:S(2)}) copy-start(f32[32,32,64]{2,1,0:T(8,128)} %sheet_ref.1) | copy-start | bytes 786436
  0.6 22.8 %copy-start.3 = (f32[32,64]{1,0:T(8,128)S(1)}, f32[32,64]{1,0:T(8,128)}, u32[]{:S(2)}) copy-start(f32[32,64]{1,0:T(8,128)} %current_ref.1) | copy-start | bytes 24580
  3.9 20.7 %copy-start = (f32[1,19,4,32,128]{4,3,2,1,0:T(8,128)S(1)}, f32[1,19,4,32,128]{4,3,2,1,0:T(8,128)}, u32[]{:S(2)}) copy-start(f32[1,19,4,32,128]{4,3,2,1,0:T(8,128)} %param.4) | copy-start | bytes 3735556
  3.9 20.7 %copy-start.2 = (s32[1,4,32,128]{3,2,1,0:T(8,128)S(1)}, s32[1,4,32,128]{3,2,1,0:T(8,128)}, u32[]{:S(2)}) copy-start(s32[1,4,32,128]{3,2,1,0:T(8,128)} %param.5) | copy-start | bytes 196612
  3.9 20.7 %collective-permute-start.2 = (f32[20,4,16,128]{3,2,1,0:T(8,128)}, f32[20,4,16,128]{3,2,1,0:T(8,128)S(1)}, u32[]{:S(2)}, u32[]{:S(2)}) collective-permute-start(f32[20,4,16,128]{3,2,1,0:T(8,128)} %get-tuple-element.14), channel_id=1, source_target_pairs={{0,4},{4,8},{8,12},{12,0},{1,5},{5,9},{9,13},{13,1},{2,6},{6,10},{... | collective-permute-start | bytes 1966088 | tf_op jit(solution)/shard_map/ppermute | solution.py:562
  6.5 18.1 %collective-permute-start.3 = (f32[20,4,16,128]{3,2,1,0:T(8,128)}, f32[20,4,16,128]{3,2,1,0:T(8,128)S(1)}, u32[]{:S(2)}, u32[]{:S(2)}) collective-permute-start(f32[20,4,16,128]{3,2,1,0:T(8,128)} %get-tuple-element.15), channel_id=1, source_target_pairs={{0,12},{4,0},{8,4},{12,8},{1,13},{5,1},{9,5},{13,9},{2,14},{6,2},{... | collective-permute-start | bytes 1966088 | tf_op jit(solution)/shard_map/ppermute | solution.py:563
  6.5 13.2 %collective-permute-start = (f32[20,16,128]{2,1,0:T(8,128)}, f32[20,16,128]{2,1,0:T(8,128)S(1)}, u32[]{:S(2)}, u32[]{:S(2)}) collective-permute-start(f32[20,16,128]{2,1,0:T(8,128)} %get-tuple-element.11), channel_id=1, source_target_pairs={{0,1},{1,2},{2,3},{3,0},{4,5},{5,6},{6,7},{7,4},{8,9},{9,10},{10,1... | collective-permute-start | bytes 491528 | tf_op jit(solution)/shard_map/ppermute | solution.py:564
  7.8 11.9 %collective-permute-start.1 = (f32[20,16,128]{2,1,0:T(8,128)}, f32[20,16,128]{2,1,0:T(8,128)S(1)}, u32[]{:S(2)}, u32[]{:S(2)}) collective-permute-start(f32[20,16,128]{2,1,0:T(8,128)} %get-tuple-element.12), channel_id=1, source_target_pairs={{0,3},{1,0},{2,1},{3,2},{4,7},{5,4},{6,5},{7,6},{8,11},{9,8},{10,9... | collective-permute-start | bytes 491528 | tf_op jit(solution)/shard_map/ppermute | solution.py:565
  19.9 7.0 %collective-permute-start.4 = (f32[22,16,128]{2,1,0:T(8,128)S(1)}, f32[22,16,128]{2,1,0:T(8,128)S(1)}, u32[]{:S(2)}, u32[]{:S(2)}) collective-permute-start(f32[22,16,128]{2,1,0:T(8,128)S(1)} %get-tuple-element.16), channel_id=1, source_target_pairs={{0,4},{4,8},{8,12},{12,0},{1,5},{5,9},{9,13},{13,1},{2,6},{6,10},{... | collective-permute-start | bytes 540680 | tf_op jit(solution)/shard_map/ppermute | solution.py:574
  23.4 5.1 %collective-permute-start.5 = (f32[22,16,128]{2,1,0:T(8,128)S(1)}, f32[22,16,128]{2,1,0:T(8,128)S(1)}, u32[]{:S(2)}, u32[]{:S(2)}) collective-permute-start(f32[22,16,128]{2,1,0:T(8,128)S(1)} %get-tuple-element.17), channel_id=1, source_target_pairs={{0,12},{4,0},{8,4},{12,8},{1,13},{5,1},{9,5},{13,9},{2,14},{6,2},{... | collective-permute-start | bytes 540680 | tf_op jit(solution)/shard_map/ppermute | solution.py:575
